TPU v7x, 512 devices: a whole 4x8x8 slice. The times are simulated.
512 devices in a mesh: seq: 16 (over x, z_lo, core), head: 32 (over z_hi, y).
Axes of the slice: x: 4, y: 8, z: 8 (z_hi: 4, z_lo: 2; z = z_hi * 2 + z_lo), core: 2. Of those that a mesh axis runs over, the one named last changes fastest.
Arguments:
- query_heads: bfloat16 [8192, 16, 128], P(('seq', 'head')), may hold values from -6 to 6
- key_heads: bfloat16 [8192, 16, 128], P(('seq', 'head')), may hold values from -6 to 6
- value_heads: bfloat16 [8192, 32, 128], P(('seq', 'head')), may hold values from -6 to 6
- gate_log: bfloat16 [8192, 32], P(('seq', 'head')), may hold values from -1 to 0
- beta_rate: bfloat16 [8192, 32], P(('seq', 'head')), may hold values from 0.0099487305 to 0.099609375
Outputs:
- head_output: bfloat16 [8192, 4096], P(('seq', 'head'))
- block_states: float32 [16, 32, 128, 128], P('seq', 'head')
All inputs are finite; a program needn't handle non-finite values.
Results may differ from a plain program's by a relative error of at most 0.001.
Values may be sent and summed in bfloat16 or wider, within the bound.
No kernel may reach another device: no remote copies, remote signals or barrier semaphores. Data moves between devices by JAX's collectives and lax.ppermute only.
A program may use at most 64 MiB of HBM per device.

v0:
```python
import jax
import jax.numpy as jnp
from jax import lax
from jax.sharding import PartitionSpec as P

STRETCH = 64


HIGHEST = lax.Precision.HIGHEST


def shifted(block, axis, distance):
    devices = range(lax.axis_size(axis))
    route = [(i - distance, i) for i in devices if i - distance in devices]
    return lax.ppermute(block, axis, route)


def normalize(tensor):
    tensor = tensor.astype(jnp.float32)
    return tensor / jnp.sqrt(jnp.sum(tensor * tensor, axis=-1, keepdims=True) + 1e-06)


def stretch_parts(queries, keys_in, values, gate_vals, beta_vals):
    span_len = gate_vals.shape[-1]
    cumulative = jnp.cumsum(gate_vals, axis=-1)
    row_ids = lax.broadcasted_iota(jnp.int32, (span_len, span_len), 0)
    columns = lax.broadcasted_iota(jnp.int32, (span_len, span_len), 1)
    strict = row_ids > columns
    inclusive = row_ids >= columns
    differ = cumulative[..., :, None] - cumulative[..., None, :]
    key_key = jnp.einsum("...rd,...sd->...rs", keys_in, keys_in, precision=HIGHEST)
    query_key = jnp.einsum("...rd,...sd->...rs", queries, keys_in, precision=HIGHEST)
    lower_triangle = jnp.where(
        strict, beta_vals[..., :, None] * jnp.exp(jnp.where(strict, differ, 0.0)) * key_key, 0.0
    )
    scores = jnp.where(inclusive, jnp.exp(jnp.where(inclusive, differ, 0.0)) * query_key, 0.0)
    identity = jnp.eye(span_len, dtype=jnp.float32)
    right_side = jnp.concatenate(
        [(beta_vals * jnp.exp(cumulative))[..., None] * keys_in, beta_vals[..., None] * values],
        axis=-1,
    )
    solved = jax.scipy.linalg.solve_triangular(
        identity + lower_triangle, right_side, lower=True, unit_diagonal=True
    )
    key_width = keys_in.shape[-1]
    last_cum = cumulative[..., -1:]
    query_dec = jnp.exp(cumulative)[..., None] * queries
    key_dec = jnp.exp(last_cum - cumulative)[..., None] * keys_in
    return (
        solved[..., :key_width],
        solved[..., key_width:],
        scores,
        query_dec,
        key_dec,
        jnp.exp(last_cum[..., 0]),
    )


def product(left_mat, right_mat):
    return jnp.einsum("...ij,...jk->...ik", left_mat, right_mat, precision=HIGHEST)


def compose(earlier, later):
    return (product(later[0], earlier[0]), product(later[0], earlier[1]) + later[1])


def slab_local(queries, keys_in, values, gate_vals, beta_vals):
    heads, length = gate_vals.shape
    blocks = length // STRETCH

    def split_rows(tensor):
        return tensor.reshape((heads, blocks, STRETCH) + tensor.shape[2:])

    write_keys, write_vals, scores, query_dec, key_dec, stretch_decay = stretch_parts(
        split_rows(queries),
        split_rows(keys_in),
        split_rows(values),
        split_rows(gate_vals),
        split_rows(beta_vals),
    )
    key_width = keys_in.shape[-1]
    identity = jnp.eye(key_width, dtype=jnp.float32)
    transit = stretch_decay[..., None, None] * identity - jnp.einsum(
        "hncd,hnce->hnde", key_dec, write_keys, precision=HIGHEST
    )
    inject = jnp.einsum("hncd,hnce->hnde", key_dec, write_vals, precision=HIGHEST)
    project = query_dec - jnp.einsum("hnrs,hnsd->hnrd", scores, write_keys, precision=HIGHEST)
    direct = jnp.einsum("hnrs,hnse->hnre", scores, write_vals, precision=HIGHEST)
    maps_all, states_all = lax.associative_scan(compose, (transit, inject), axis=1)
    reach_rest = product(project[:, 1:], maps_all[:, :-1])
    reach = jnp.concatenate([project[:, :1], reach_rest], axis=1).reshape(heads, length, key_width)
    out_rest = product(project[:, 1:], states_all[:, :-1]) + direct[:, 1:]
    local_out = jnp.concatenate([direct[:, :1], out_rest], axis=1).reshape(heads, length, -1)
    return (local_out, reach, maps_all[:, -1], states_all[:, -1])


def per_device(query_heads, key_heads, value_heads, gate_log, beta_rate):
    key_count = query_heads.shape[1]
    grouping = value_heads.shape[1] // key_count
    got_query, got_key, got_value, got_gate, got_beta = (
        lax.all_to_all(
            jnp.repeat(query_heads, grouping, axis=1),
            "head",
            split_axis=1,
            concat_axis=0,
            tiled=True,
        ),
        lax.all_to_all(
            jnp.repeat(key_heads, grouping, axis=1), "head", split_axis=1, concat_axis=0, tiled=True
        ),
        lax.all_to_all(value_heads, "head", split_axis=1, concat_axis=0, tiled=True),
        lax.all_to_all(gate_log, "head", split_axis=1, concat_axis=0, tiled=True),
        lax.all_to_all(beta_rate, "head", split_axis=1, concat_axis=0, tiled=True),
    )
    queries = jnp.swapaxes(normalize(got_query), 0, 1)
    keys_in = jnp.swapaxes(normalize(got_key), 0, 1)
    values = jnp.swapaxes(got_value.astype(jnp.float32), 0, 1)
    gate_vals = jnp.swapaxes(got_gate.astype(jnp.float32), 0, 1)
    beta_vals = jnp.swapaxes(got_beta.astype(jnp.float32), 0, 1)
    local_out, reach, slab_map, slab_state = slab_local(
        queries, keys_in, values, gate_vals, beta_vals
    )

    def advance(counter, carried):
        return shifted(product(slab_map, carried) + slab_state, "seq", 1)

    incoming = lax.fori_loop(0, lax.axis_size("seq") - 1, advance, jnp.zeros_like(slab_state))
    combined = local_out + product(reach, incoming)
    head_rows = jnp.swapaxes(combined, 0, 1).astype(jnp.bfloat16)
    flat_rows = head_rows.reshape(head_rows.shape[0], -1)
    head_output = lax.all_to_all(flat_rows, "head", split_axis=0, concat_axis=1, tiled=True)
    last_state = (product(slab_map, incoming) + slab_state)[None]
    return (head_output, last_state)


def solution(mesh):
    return jax.shard_map(
        per_device,
        mesh=mesh,
        in_specs=(
            P(("seq", "head"), None, None),
            P(("seq", "head"), None, None),
            P(("seq", "head"), None, None),
            P(("seq", "head"), None),
            P(("seq", "head"), None),
        ),
        out_specs=(P(("seq", "head"), None), P("seq", "head", None, None)),
        check_vma=False,
    )
```

profile of v0, /device:TPU:4, one launch (start us, length us, event | category | flops | bytes accessed | tf_op | source)
XLA Modules:
  0.0 271.3 jit_solution(10966988010122884502)
XLA Ops:
  0.6 1.4 copy.27
  2.0 16.0 %all-to-all-start = ((bf16[16,32,1]{0,2,1:T(2,128)(2,1)}), bf16[16,32,1]{0,2,1:T(2,128)(2,1)S(1)}, u32[]{:S(2)}, u32[]{:S(2)}) async-start(bf16[16,32,1]{0,2,1:T(2,128)(2,1)} %copy.27), calls=%async_computation | async-start | bytes 32768 | tf_op jit(solution)/shard_map/all_to_all | solution.py:112
  21.1 9.0 %all-to-all-done = bf16[16,32,1]{0,2,1:T(2,128)(2,1)S(1)} async-done(((bf16[16,32,1]{0,2,1:T(2,128)(2,1)}), bf16[16,32,1]{0,2,1:T(2,128)(2,1)S(1)}, u32[]{:S(2)}, u32[]{:S(2)}) %all-to-all-start) | async-done | bytes 1056 | tf_op jit(solution)/shard_map/all_to_all | solution.py:112
  30.1 3.8 %all-to-all-start.3 = ((bf16[16,32,1]{0,2,1:T(2,128)(2,1)}), bf16[16,32,1]{0,2,1:T(2,128)(2,1)S(1)}, u32[]{:S(2)}, u32[]{:S(2)}) async-start(bf16[16,32,1]{0,2,1:T(2,128)(2,1)} %copy.30), calls=%async_computation.3 | async-start | bytes 32768 | tf_op jit(solution)/shard_map/all_to_all | solution.py:113
  34.3 11.8 %all-to-all-done.3 = bf16[16,32,1]{0,2,1:T(2,128)(2,1)S(1)} async-done(((bf16[16,32,1]{0,2,1:T(2,128)(2,1)}), bf16[16,32,1]{0,2,1:T(2,128)(2,1)S(1)}, u32[]{:S(2)}, u32[]{:S(2)}) %all-to-all-start.3) | async-done | bytes 1056 | tf_op jit(solution)/shard_map/all_to_all | solution.py:113
  46.8 3.8 %all-to-all-start.2 = ((bf16[16,32,128]{2,0,1:T(8,128)(2,1)}), bf16[16,32,128]{2,0,1:T(8,128)(2,1)S(1)}, u32[]{:S(2)}, u32[]{:S(2)}) async-start(bf16[16,32,128]{2,0,1:T(8,128)(2,1)} %bitcast.12), calls=%async_computation.2 | async-start | bytes 262144 | tf_op jit(solution)/shard_map/all_to_all | solution.py:108
  51.6 11.8 %all-to-all-done.2 = bf16[16,32,128]{2,0,1:T(8,128)(2,1)S(1)} async-done(((bf16[16,32,128]{2,0,1:T(8,128)(2,1)}), bf16[16,32,128]{2,0,1:T(8,128)(2,1)S(1)}, u32[]{:S(2)}, u32[]{:S(2)}) %all-to-all-start.2) | async-done | bytes 131104 | tf_op jit(solution)/shard_map/all_to_all | solution.py:108
  63.4 3.9 %all-to-all-start.4 = ((bf16[16,32,128]{2,0,1:T(8,128)(2,1)}), bf16[16,32,128]{2,0,1:T(8,128)(2,1)S(1)}, u32[]{:S(2)}, u32[]{:S(2)}) async-start(bf16[16,32,128]{2,0,1:T(8,128)(2,1)} %copy.31), calls=%async_computation.4 | async-start | bytes 262144 | tf_op jit(solution)/shard_map/all_to_all | solution.py:111
  67.5 12.5 %all-to-all-done.4 = bf16[16,32,128]{2,0,1:T(8,128)(2,1)S(1)} async-done(((bf16[16,32,128]{2,0,1:T(8,128)(2,1)}), bf16[16,32,128]{2,0,1:T(8,128)(2,1)S(1)}, u32[]{:S(2)}, u32[]{:S(2)}) %all-to-all-start.4) | async-done | bytes 131104 | tf_op jit(solution)/shard_map/all_to_all | solution.py:111
  80.7 4.0 %all-to-all-start.1 = ((bf16[16,32,128]{2,0,1:T(8,128)(2,1)}), bf16[16,32,128]{2,0,1:T(8,128)(2,1)S(1)}, u32[]{:S(2)}, u32[]{:S(2)}) async-start(bf16[16,32,128]{2,0,1:T(8,128)(2,1)} %bitcast.7), calls=%async_computation.1 | async-start | bytes 262144 | tf_op jit(solution)/shard_map/all_to_all | solution.py:101
  85.6 39.3 %custom-call.4 = f32[8,1,64,64]{2,3,1,0:T(8,128)S(1)} custom-call(f32[8,1,64,64]{3,2,1,0:T(8,128)S(1)} %fusion.10), custom_call_target="InvertDiagBlocksLowerTriangular" | custom-call | tf_op jit(solution)/shard_map/jit(_solve_triangular)/vmap()/triangular_solve | solution.py:42
  127.0 1.2 fusion.3
  132.8 2.1 pad.117
  135.0 2.1 pad.115
  137.1 1.3 fusion.14
  144.4 100.4 %while.10 = (s32[]{:T(128)}, f32[1,128,128]{2,1,0:T(8,128)S(1)}, f32[1,128,128]{2,1,0:T(8,128)S(1)}, f32[1,128,128]{2,1,0:T(8,128)S(1)}, s32[]{:T(128)}) while((s32[]{:T(128)}, f32[1,128,128]{2,1,0:T(8,128)S(1)}, f32[1,128,128]{2,1,0:T(8,128)S(1)}, f32[1,128,128]{2,1,0:T(8,128)S(1)}, s32[]{:T(128)}) %tuple.30), condition=%wide.region_4.5_spmd, body=%wide.region_3.4_spmd.sunk | while | flops 25182208 | bytes 524389 | solution.py:127
  144.6 1.9 collective-permute-start
  146.6 4.6 %collective-permute-done = f32[1,128,128]{2,1,0:T(8,128)S(1)} collective-permute-done((f32[1,128,128]{2,1,0:T(8,128)S(1)}, f32[1,128,128]{2,1,0:T(8,128)S(1)}, u32[]{:S(2)}, u32[]{:S(2)}) %collective-permute-start) | collective-permute-done | bytes 65568 | tf_op jit(solution)/shard_map/while/body/eval_jaxpr/ppermute | solution.py:15
  151.3 1.9 collective-permute-start
  153.2 4.6 %collective-permute-done = f32[1,128,128]{2,1,0:T(8,128)S(1)} collective-permute-done((f32[1,128,128]{2,1,0:T(8,128)S(1)}, f32[1,128,128]{2,1,0:T(8,128)S(1)}, u32[]{:S(2)}, u32[]{:S(2)}) %collective-permute-start) | collective-permute-done | bytes 65568 | tf_op jit(solution)/shard_map/while/body/eval_jaxpr/ppermute | solution.py:15
  158.0 1.9 collective-permute-start
  159.9 4.6 %collective-permute-done = f32[1,128,128]{2,1,0:T(8,128)S(1)} collective-permute-done((f32[1,128,128]{2,1,0:T(8,128)S(1)}, f32[1,128,128]{2,1,0:T(8,128)S(1)}, u32[]{:S(2)}, u32[]{:S(2)}) %collective-permute-start) | collective-permute-done | bytes 65568 | tf_op jit(solution)/shard_map/while/body/eval_jaxpr/ppermute | solution.py:15
  164.7 1.9 collective-permute-start
  166.6 4.6 %collective-permute-done = f32[1,128,128]{2,1,0:T(8,128)S(1)} collective-permute-done((f32[1,128,128]{2,1,0:T(8,128)S(1)}, f32[1,128,128]{2,1,0:T(8,128)S(1)}, u32[]{:S(2)}, u32[]{:S(2)}) %collective-permute-start) | collective-permute-done | bytes 65568 | tf_op jit(solution)/shard_map/while/body/eval_jaxpr/ppermute | solution.py:15
  171.4 1.9 collective-permute-start
  173.3 4.6 %collective-permute-done = f32[1,128,128]{2,1,0:T(8,128)S(1)} collective-permute-done((f32[1,128,128]{2,1,0:T(8,128)S(1)}, f32[1,128,128]{2,1,0:T(8,128)S(1)}, u32[]{:S(2)}, u32[]{:S(2)}) %collective-permute-start) | collective-permute-done | bytes 65568 | tf_op jit(solution)/shard_map/while/body/eval_jaxpr/ppermute | solution.py:15
  178.1 1.9 collective-permute-start
  180.0 4.6 %collective-permute-done = f32[1,128,128]{2,1,0:T(8,128)S(1)} collective-permute-done((f32[1,128,128]{2,1,0:T(8,128)S(1)}, f32[1,128,128]{2,1,0:T(8,128)S(1)}, u32[]{:S(2)}, u32[]{:S(2)}) %collective-permute-start) | collective-permute-done | bytes 65568 | tf_op jit(solution)/shard_map/while/body/eval_jaxpr/ppermute | solution.py:15
  184.8 1.9 collective-permute-start
  186.7 4.6 %collective-permute-done = f32[1,128,128]{2,1,0:T(8,128)S(1)} collective-permute-done((f32[1,128,128]{2,1,0:T(8,128)S(1)}, f32[1,128,128]{2,1,0:T(8,128)S(1)}, u32[]{:S(2)}, u32[]{:S(2)}) %collective-permute-start) | collective-permute-done | bytes 65568 | tf_op jit(solution)/shard_map/while/body/eval_jaxpr/ppermute | solution.py:15
  191.5 1.9 collective-permute-start
  193.4 4.6 %collective-permute-done = f32[1,128,128]{2,1,0:T(8,128)S(1)} collective-permute-done((f32[1,128,128]{2,1,0:T(8,128)S(1)}, f32[1,128,128]{2,1,0:T(8,128)S(1)}, u32[]{:S(2)}, u32[]{:S(2)}) %collective-permute-start) | collective-permute-done | bytes 65568 | tf_op jit(solution)/shard_map/while/body/eval_jaxpr/ppermute | solution.py:15
  198.2 1.9 collective-permute-start
  200.1 4.6 %collective-permute-done = f32[1,128,128]{2,1,0:T(8,128)S(1)} collective-permute-done((f32[1,128,128]{2,1,0:T(8,128)S(1)}, f32[1,128,128]{2,1,0:T(8,128)S(1)}, u32[]{:S(2)}, u32[]{:S(2)}) %collective-permute-start) | collective-permute-done | bytes 65568 | tf_op jit(solution)/shard_map/while/body/eval_jaxpr/ppermute | solution.py:15
  204.9 1.9 collective-permute-start
  206.8 4.6 %collective-permute-done = f32[1,128,128]{2,1,0:T(8,128)S(1)} collective-permute-done((f32[1,128,128]{2,1,0:T(8,128)S(1)}, f32[1,128,128]{2,1,0:T(8,128)S(1)}, u32[]{:S(2)}, u32[]{:S(2)}) %collective-permute-start) | collective-permute-done | bytes 65568 | tf_op jit(solution)/shard_map/while/body/eval_jaxpr/ppermute | solution.py:15
  211.6 1.9 collective-permute-start
  213.5 4.6 %collective-permute-done = f32[1,128,128]{2,1,0:T(8,128)S(1)} collective-permute-done((f32[1,128,128]{2,1,0:T(8,128)S(1)}, f32[1,128,128]{2,1,0:T(8,128)S(1)}, u32[]{:S(2)}, u32[]{:S(2)}) %collective-permute-start) | collective-permute-done | bytes 65568 | tf_op jit(solution)/shard_map/while/body/eval_jaxpr/ppermute | solution.py:15
  218.3 1.9 collective-permute-start
  220.2 4.6 %collective-permute-done = f32[1,128,128]{2,1,0:T(8,128)S(1)} collective-permute-done((f32[1,128,128]{2,1,0:T(8,128)S(1)}, f32[1,128,128]{2,1,0:T(8,128)S(1)}, u32[]{:S(2)}, u32[]{:S(2)}) %collective-permute-start) | collective-permute-done | bytes 65568 | tf_op jit(solution)/shard_map/while/body/eval_jaxpr/ppermute | solution.py:15
  225.0 1.9 collective-permute-start
  226.9 4.6 %collective-permute-done = f32[1,128,128]{2,1,0:T(8,128)S(1)} collective-permute-done((f32[1,128,128]{2,1,0:T(8,128)S(1)}, f32[1,128,128]{2,1,0:T(8,128)S(1)}, u32[]{:S(2)}, u32[]{:S(2)}) %collective-permute-start) | collective-permute-done | bytes 65568 | tf_op jit(solution)/shard_map/while/body/eval_jaxpr/ppermute | solution.py:15
  231.7 1.9 collective-permute-start
  233.6 4.6 %collective-permute-done = f32[1,128,128]{2,1,0:T(8,128)S(1)} collective-permute-done((f32[1,128,128]{2,1,0:T(8,128)S(1)}, f32[1,128,128]{2,1,0:T(8,128)S(1)}, u32[]{:S(2)}, u32[]{:S(2)}) %collective-permute-start) | collective-permute-done | bytes 65568 | tf_op jit(solution)/shard_map/while/body/eval_jaxpr/ppermute | solution.py:15
  238.3 1.9 collective-permute-start
  240.3 4.6 %collective-permute-done = f32[1,128,128]{2,1,0:T(8,128)S(1)} collective-permute-done((f32[1,128,128]{2,1,0:T(8,128)S(1)}, f32[1,128,128]{2,1,0:T(8,128)S(1)}, u32[]{:S(2)}, u32[]{:S(2)}) %collective-permute-start) | collective-permute-done | bytes 65568 | tf_op jit(solution)/shard_map/while/body/eval_jaxpr/ppermute | solution.py:15
  245.9 12.0 %all-to-all-start.5 = ((bf16[32,16,128]{2,1,0:T(8,128)(2,1)}), bf16[32,16,128]{2,1,0:T(8,128)(2,1)S(1)}, u32[]{:S(2)}, u32[]{:S(2)}) async-start(bf16[32,16,128]{2,1,0:T(8,128)(2,1)} %bitcast.69), calls=%async_computation.5 | async-start | bytes 262144 | tf_op jit(solution)/shard_map/all_to_all | solution.py:131
  258.7 11.9 %all-to-all-done.5 = bf16[32,16,128]{2,1,0:T(8,128)(2,1)S(1)} async-done(((bf16[32,16,128]{2,1,0:T(8,128)(2,1)}), bf16[32,16,128]{2,1,0:T(8,128)(2,1)S(1)}, u32[]{:S(2)}, u32[]{:S(2)}) %all-to-all-start.5) | async-done | bytes 131104 | tf_op jit(solution)/shard_map/all_to_all | solution.py:131
  (118 shorter events, 24.8 us)
Async XLA Ops:
  2.0 28.1 %all-to-all-start = ((bf16[16,32,1]{0,2,1:T(2,128)(2,1)}), bf16[16,32,1]{0,2,1:T(2,128)(2,1)S(1)}, u32[]{:S(2)}, u32[]{:S(2)}) async-start(bf16[16,32,1]{0,2,1:T(2,128)(2,1)} %copy.27), calls=%async_computation | async-start | bytes 32768 | tf_op jit(solution)/shard_map/all_to_all | solution.py:112
  18.0 1.5 copy-start.6
  18.1 0.7 copy-start.8
  18.8 0.8 copy-start.7
  19.5 0.9 copy-start.5
  30.1 16.0 %all-to-all-start.3 = ((bf16[16,32,1]{0,2,1:T(2,128)(2,1)}), bf16[16,32,1]{0,2,1:T(2,128)(2,1)S(1)}, u32[]{:S(2)}, u32[]{:S(2)}) async-start(bf16[16,32,1]{0,2,1:T(2,128)(2,1)} %copy.30), calls=%async_computation.3 | async-start | bytes 32768 | tf_op jit(solution)/shard_map/all_to_all | solution.py:113
  46.8 16.6 %all-to-all-start.2 = ((bf16[16,32,128]{2,0,1:T(8,128)(2,1)}), bf16[16,32,128]{2,0,1:T(8,128)(2,1)S(1)}, u32[]{:S(2)}, u32[]{:S(2)}) async-start(bf16[16,32,128]{2,0,1:T(8,128)(2,1)} %bitcast.12), calls=%async_computation.2 | async-start | bytes 262144 | tf_op jit(solution)/shard_map/all_to_all | solution.py:108
  63.4 16.6 %all-to-all-start.4 = ((bf16[16,32,128]{2,0,1:T(8,128)(2,1)}), bf16[16,32,128]{2,0,1:T(8,128)(2,1)S(1)}, u32[]{:S(2)}, u32[]{:S(2)}) async-start(bf16[16,32,128]{2,0,1:T(8,128)(2,1)} %copy.31), calls=%async_computation.4 | async-start | bytes 262144 | tf_op jit(solution)/shard_map/all_to_all | solution.py:111
  80.7 57.7 %all-to-all-start.1 = ((bf16[16,32,128]{2,0,1:T(8,128)(2,1)}), bf16[16,32,128]{2,0,1:T(8,128)(2,1)S(1)}, u32[]{:S(2)}, u32[]{:S(2)}) async-start(bf16[16,32,128]{2,0,1:T(8,128)(2,1)} %bitcast.7), calls=%async_computation.1 | async-start | bytes 262144 | tf_op jit(solution)/shard_map/all_to_all | solution.py:101
  127.0 5.6 %copy-start.4 = (f32[1,8,128,128]{3,2,1,0:T(8,128)}, f32[1,8,128,128]{3,2,1,0:T(8,128)S(1)}, u32[]{:S(2)}) copy-start(f32[1,8,128,128]{3,2,1,0:T(8,128)S(1)} %convolution_bitcast_fusion) | copy-start | bytes 1572868
  128.2 9.0 %copy-start = (f32[1,8,128,128]{3,2,1,0:T(8,128)}, f32[1,8,128,128]{3,2,1,0:T(8,128)S(1)}, u32[]{:S(2)}) copy-start(f32[1,8,128,128]{3,2,1,0:T(8,128)S(1)} %fusion.3) | copy-start | bytes 1572868
  128.6 1.7 copy-start.1
  129.7 0.7 copy-start.2
  130.6 0.8 slice-start.1
  131.6 1.0 slice-start.2
  139.3 0.7 copy-start.9
  140.4 0.8 slice-start.3
  141.3 0.8 slice-start
  141.3 1.0 copy-start.3
  144.6 6.5 %collective-permute-start = (f32[1,128,128]{2,1,0:T(8,128)S(1)}, f32[1,128,128]{2,1,0:T(8,128)S(1)}, u32[]{:S(2)}, u32[]{:S(2)}) collective-permute-start(f32[1,128,128]{2,1,0:T(8,128)S(1)} %fusion.89), channel_id=1, source_target_pairs={{0,32},{32,64},{64,96},{96,128},{128,160},{160,192},{192,224},{224... | collective-permute-start | bytes 196616 | tf_op jit(solution)/shard_map/while/body/eval_jaxpr/ppermute | solution.py:15
  151.3 6.5 %collective-permute-start = (f32[1,128,128]{2,1,0:T(8,128)S(1)}, f32[1,128,128]{2,1,0:T(8,128)S(1)}, u32[]{:S(2)}, u32[]{:S(2)}) collective-permute-start(f32[1,128,128]{2,1,0:T(8,128)S(1)} %fusion.89), channel_id=1, source_target_pairs={{0,32},{32,64},{64,96},{96,128},{128,160},{160,192},{192,224},{224... | collective-permute-start | bytes 196616 | tf_op jit(solution)/shard_map/while/body/eval_jaxpr/ppermute | solution.py:15
  158.0 6.5 %collective-permute-start = (f32[1,128,128]{2,1,0:T(8,128)S(1)}, f32[1,128,128]{2,1,0:T(8,128)S(1)}, u32[]{:S(2)}, u32[]{:S(2)}) collective-permute-start(f32[1,128,128]{2,1,0:T(8,128)S(1)} %fusion.89), channel_id=1, source_target_pairs={{0,32},{32,64},{64,96},{96,128},{128,160},{160,192},{192,224},{224... | collective-permute-start | bytes 196616 | tf_op jit(solution)/shard_map/while/body/eval_jaxpr/ppermute | solution.py:15
  164.7 6.5 %collective-permute-start = (f32[1,128,128]{2,1,0:T(8,128)S(1)}, f32[1,128,128]{2,1,0:T(8,128)S(1)}, u32[]{:S(2)}, u32[]{:S(2)}) collective-permute-start(f32[1,128,128]{2,1,0:T(8,128)S(1)} %fusion.89), channel_id=1, source_target_pairs={{0,32},{32,64},{64,96},{96,128},{128,160},{160,192},{192,224},{224... | collective-permute-start | bytes 196616 | tf_op jit(solution)/shard_map/while/body/eval_jaxpr/ppermute | solution.py:15
  171.4 6.5 %collective-permute-start = (f32[1,128,128]{2,1,0:T(8,128)S(1)}, f32[1,128,128]{2,1,0:T(8,128)S(1)}, u32[]{:S(2)}, u32[]{:S(2)}) collective-permute-start(f32[1,128,128]{2,1,0:T(8,128)S(1)} %fusion.89), channel_id=1, source_target_pairs={{0,32},{32,64},{64,96},{96,128},{128,160},{160,192},{192,224},{224... | collective-permute-start | bytes 196616 | tf_op jit(solution)/shard_map/while/body/eval_jaxpr/ppermute | solution.py:15
  178.1 6.5 %collective-permute-start = (f32[1,128,128]{2,1,0:T(8,128)S(1)}, f32[1,128,128]{2,1,0:T(8,128)S(1)}, u32[]{:S(2)}, u32[]{:S(2)}) collective-permute-start(f32[1,128,128]{2,1,0:T(8,128)S(1)} %fusion.89), channel_id=1, source_target_pairs={{0,32},{32,64},{64,96},{96,128},{128,160},{160,192},{192,224},{224... | collective-permute-start | bytes 196616 | tf_op jit(solution)/shard_map/while/body/eval_jaxpr/ppermute | solution.py:15
  184.8 6.5 %collective-permute-start = (f32[1,128,128]{2,1,0:T(8,128)S(1)}, f32[1,128,128]{2,1,0:T(8,128)S(1)}, u32[]{:S(2)}, u32[]{:S(2)}) collective-permute-start(f32[1,128,128]{2,1,0:T(8,128)S(1)} %fusion.89), channel_id=1, source_target_pairs={{0,32},{32,64},{64,96},{96,128},{128,160},{160,192},{192,224},{224... | collective-permute-start | bytes 196616 | tf_op jit(solution)/shard_map/while/body/eval_jaxpr/ppermute | solution.py:15
  191.5 6.5 %collective-permute-start = (f32[1,128,128]{2,1,0:T(8,128)S(1)}, f32[1,128,128]{2,1,0:T(8,128)S(1)}, u32[]{:S(2)}, u32[]{:S(2)}) collective-permute-start(f32[1,128,128]{2,1,0:T(8,128)S(1)} %fusion.89), channel_id=1, source_target_pairs={{0,32},{32,64},{64,96},{96,128},{128,160},{160,192},{192,224},{224... | collective-permute-start | bytes 196616 | tf_op jit(solution)/shard_map/while/body/eval_jaxpr/ppermute | solution.py:15
  198.2 6.5 %collective-permute-start = (f32[1,128,128]{2,1,0:T(8,128)S(1)}, f32[1,128,128]{2,1,0:T(8,128)S(1)}, u32[]{:S(2)}, u32[]{:S(2)}) collective-permute-start(f32[1,128,128]{2,1,0:T(8,128)S(1)} %fusion.89), channel_id=1, source_target_pairs={{0,32},{32,64},{64,96},{96,128},{128,160},{160,192},{192,224},{224... | collective-permute-start | bytes 196616 | tf_op jit(solution)/shard_map/while/body/eval_jaxpr/ppermute | solution.py:15
  204.9 6.5 %collective-permute-start = (f32[1,128,128]{2,1,0:T(8,128)S(1)}, f32[1,128,128]{2,1,0:T(8,128)S(1)}, u32[]{:S(2)}, u32[]{:S(2)}) collective-permute-start(f32[1,128,128]{2,1,0:T(8,128)S(1)} %fusion.89), channel_id=1, source_target_pairs={{0,32},{32,64},{64,96},{96,128},{128,160},{160,192},{192,224},{224... | collective-permute-start | bytes 196616 | tf_op jit(solution)/shard_map/while/body/eval_jaxpr/ppermute | solution.py:15
  211.6 6.5 %collective-permute-start = (f32[1,128,128]{2,1,0:T(8,128)S(1)}, f32[1,128,128]{2,1,0:T(8,128)S(1)}, u32[]{:S(2)}, u32[]{:S(2)}) collective-permute-start(f32[1,128,128]{2,1,0:T(8,128)S(1)} %fusion.89), channel_id=1, source_target_pairs={{0,32},{32,64},{64,96},{96,128},{128,160},{160,192},{192,224},{224... | collective-permute-start | bytes 196616 | tf_op jit(solution)/shard_map/while/body/eval_jaxpr/ppermute | solution.py:15
  218.3 6.5 %collective-permute-start = (f32[1,128,128]{2,1,0:T(8,128)S(1)}, f32[1,128,128]{2,1,0:T(8,128)S(1)}, u32[]{:S(2)}, u32[]{:S(2)}) collective-permute-start(f32[1,128,128]{2,1,0:T(8,128)S(1)} %fusion.89), channel_id=1, source_target_pairs={{0,32},{32,64},{64,96},{96,128},{128,160},{160,192},{192,224},{224... | collective-permute-start | bytes 196616 | tf_op jit(solution)/shard_map/while/body/eval_jaxpr/ppermute | solution.py:15
  225.0 6.5 %collective-permute-start = (f32[1,128,128]{2,1,0:T(8,128)S(1)}, f32[1,128,128]{2,1,0:T(8,128)S(1)}, u32[]{:S(2)}, u32[]{:S(2)}) collective-permute-start(f32[1,128,128]{2,1,0:T(8,128)S(1)} %fusion.89), channel_id=1, source_target_pairs={{0,32},{32,64},{64,96},{96,128},{128,160},{160,192},{192,224},{224... | collective-permute-start | bytes 196616 | tf_op jit(solution)/shard_map/while/body/eval_jaxpr/ppermute | solution.py:15
  231.7 6.5 %collective-permute-start = (f32[1,128,128]{2,1,0:T(8,128)S(1)}, f32[1,128,128]{2,1,0:T(8,128)S(1)}, u32[]{:S(2)}, u32[]{:S(2)}) collective-permute-start(f32[1,128,128]{2,1,0:T(8,128)S(1)} %fusion.89), channel_id=1, source_target_pairs={{0,32},{32,64},{64,96},{96,128},{128,160},{160,192},{192,224},{224... | collective-permute-start | bytes 196616 | tf_op jit(solution)/shard_map/while/body/eval_jaxpr/ppermute | solution.py:15
  238.3 6.5 %collective-permute-start = (f32[1,128,128]{2,1,0:T(8,128)S(1)}, f32[1,128,128]{2,1,0:T(8,128)S(1)}, u32[]{:S(2)}, u32[]{:S(2)}) collective-permute-start(f32[1,128,128]{2,1,0:T(8,128)S(1)} %fusion.89), channel_id=1, source_target_pairs={{0,32},{32,64},{64,96},{96,128},{128,160},{160,192},{192,224},{224... | collective-permute-start | bytes 196616 | tf_op jit(solution)/shard_map/while/body/eval_jaxpr/ppermute | solution.py:15
  245.9 24.8 %all-to-all-start.5 = ((bf16[32,16,128]{2,1,0:T(8,128)(2,1)}), bf16[32,16,128]{2,1,0:T(8,128)(2,1)S(1)}, u32[]{:S(2)}, u32[]{:S(2)}) async-start(bf16[32,16,128]{2,1,0:T(8,128)(2,1)} %bitcast.69), calls=%async_computation.5 | async-start | bytes 262144 | tf_op jit(solution)/shard_map/all_to_all | solution.py:131
where the time goes:
time: 272 us; the launch traced here: 271 us
  waiting for transfers between devices  125 us (46%)
  starting transfers between devices  72.3 us (27%)
  other arithmetic  42.1 us (15%)
  matrix products  15.5 us (6%)
  local copies, waits for them, and re-layouts  14.5 us (5%)
    ppermute x15, waiting for transfers between devices, shifted(): return lax.ppermute(block, axis, route)  68.3 us
    another operation x2, other arithmetic, stretch_parts(): jax.scipy.linalg.solve_triangular(identity + lower_triangle, right_side,...  39.3 us
    ppermute x15, starting transfers between devices, shifted(): return lax.ppermute(block, axis, route)  28.8 us
    all_to_all x1, starting transfers between devices, per_device(): lax.all_to_all(gate_log, 'head', split_axis=1, concat_axis=0, tiled=True)  16 us
    all_to_all x1, waiting for transfers between devices, per_device(): lax.all_to_all(value_heads, 'head', split_axis=1, concat_axis=0, tiled=True)  12.5 us
    all_to_all x1, starting transfers between devices, per_device(): lax.all_to_all(flat_rows, 'head', split_axis=0, concat_axis=1, tiled=True)  12 us
    all_to_all x1, waiting for transfers between devices, per_device(): lax.all_to_all(flat_rows, 'head', split_axis=0, concat_axis=1, tiled=True)  11.9 us
    all_to_all x1, waiting for transfers between devices, per_device(): lax.all_to_all(jnp.repeat(key_heads, grouping, axis=1), 'head', split_axi...  11.8 us
  transfers between devices with their start and end apart: 21, of which 20 were waited for; matrix products, arithmetic and copies ran while one was open for 21% of the time, Pallas kernels for 0%

commit v1 on v0

v1 whole, which is shorter than its diff:
```python
import jax
import jax.numpy as jnp
from jax import lax
from jax.experimental import pallas as pl
from jax.experimental.pallas import tpu as pltpu
from jax.sharding import PartitionSpec as P

F32 = jnp.float32
BF16 = jnp.bfloat16
TOK = 512
DIM = 128
SRC = 32
PER = 16
HALF = 256


def iota(shape, dim):
    return lax.broadcasted_iota(jnp.int32, shape, dim)


def dot1(a, b):
    return lax.dot_general(a, b, (((1,), (0,)), ((), ())), preferred_element_type=F32)


def dot_t(a, b):
    return lax.dot_general(a, b, (((1,), (1,)), ((), ())), preferred_element_type=F32)


def split(a):
    high = a.astype(BF16)
    return high, (a - high.astype(F32)).astype(BF16)


def dot3(a, b):
    ah, al = split(a)
    bh, bl = split(b)
    return dot1(ah, bh) + (dot1(ah, bl) + dot1(al, bh))


def inv_norm(total):
    total = total + 1e-6
    y = lax.rsqrt(total)
    return y * (1.5 - 0.5 * total * y * y)


def row_sums(x):
    squares = x.astype(F32) * x.astype(F32)
    column = jnp.sum(squares, axis=1, keepdims=True)
    high, low = split(squares)
    ones = jnp.ones((8, DIM), BF16)
    row = (dot_t(ones, high) + dot_t(ones, low))[0:1]
    return column, row


def columns_of(got_ref):
    extra = got_ref[:, 48:56, :].astype(F32)
    lanes = extra[:, 0, :].astype(BF16)
    spread = (iota((TOK, SRC), 0) // PER == iota((TOK, SRC), 1)).astype(F32).astype(BF16)
    rows = dot1(spread, lanes)
    lane = iota((TOK, DIM), 1)
    spot = iota((TOK, DIM), 0) % PER
    gate = jnp.sum(jnp.where(lane == spot, rows, 0.0), axis=1, keepdims=True)
    beta = jnp.sum(jnp.where(lane == spot + PER, rows, 0.0), axis=1, keepdims=True)
    return gate, beta


def spans(gate):
    row, col = iota((TOK, TOK), 0), iota((TOK, TOK), 1)
    upto = (row >= col).astype(F32).astype(BF16)
    after = jnp.where(row > col, gate, 0.0).astype(BF16)
    return dot1(upto, after), row, col, upto


def local_kernel(got_ref, pair_ref, solved_ref):
    gate, beta = columns_of(got_ref)
    keys = got_ref[:, 16:32, :].reshape(TOK, DIM)
    values = got_ref[:, 32:48, :].reshape(TOK, DIM)
    differ, row, col, upto = spans(gate)
    k_col, k_row = row_sums(keys)
    inv_col, inv_row = inv_norm(k_col), inv_norm(k_row)
    key_key = dot_t(keys, keys)
    strict = row > col
    lower = jnp.where(
        strict, (beta * inv_col) * jnp.exp(jnp.where(strict, differ, 0.0)) * key_key * inv_row, 0.0
    )
    gate_wide = jnp.broadcast_to(gate, (TOK, DIM)).astype(BF16)
    cumul = dot1(upto, gate_wide)
    tail = jnp.sum(gate_wide.astype(F32), axis=0, keepdims=True)
    beyond = dot1((row < col).astype(F32).astype(BF16), gate_wide)
    right = jnp.concatenate(
        [
            (beta * inv_col) * jnp.exp(cumul) * keys.astype(F32),
            beta * values.astype(F32),
        ],
        axis=1,
    )
    r, c = iota((HALF, HALF), 0), iota((HALF, HALF), 1)
    inverses = []
    for part in range(2):
        block = lower[part * HALF : (part + 1) * HALF, part * HALF : (part + 1) * HALF]
        eye = jnp.where(r == c, 1.0, 0.0)
        n1 = jnp.where(r // 16 == c // 16, -block, 0.0)
        n2 = dot3(n1, n1)
        x = eye + n1 + n2 + dot3(n1, n2)
        n4 = dot3(n2, n2)
        x = x + dot3(x, n4)
        n8 = dot3(n4, n4)
        x = x + dot3(x, n8)
        for width in (16, 32, 64, 128):
            here = (r // (2 * width) == c // (2 * width)) & (r // width != c // width)
            x = x - dot3(x, dot3(jnp.where(here, block, 0.0), x))
        inverses.append(x)
    top = dot3(inverses[0], right[:HALF])
    bottom = dot3(inverses[1], right[HALF:] - dot3(lower[HALF:, :HALF], top))
    solved = jnp.concatenate([top, bottom], axis=0)
    solved_ref[...] = solved
    weight = inv_col * jnp.exp(beyond)
    scaled = jnp.concatenate([weight, weight], axis=1) * solved
    high, low = split(scaled)
    keys_t = keys.T
    moved = dot1(keys_t, high) + dot1(keys_t, low)
    d_row, d_col = iota((DIM, DIM), 0), iota((DIM, DIM), 1)
    carry = jnp.where(d_row == d_col, jnp.exp(tail), 0.0)
    pair_ref[:, :DIM] = carry - moved[:, :DIM]
    pair_ref[:, DIM:] = moved[:, DIM:]


def readout_kernel(got_ref, solved_ref, direct_ref, reach_ref):
    gate, _ = columns_of(got_ref)
    queries = got_ref[:, 0:16, :].reshape(TOK, DIM)
    keys = got_ref[:, 16:32, :].reshape(TOK, DIM)
    differ, row, col, upto = spans(gate)
    q_col, _ = row_sums(queries)
    _, k_row = row_sums(keys)
    query_inv = inv_norm(q_col)
    inclusive = row >= col
    scores = jnp.where(
        inclusive,
        query_inv * jnp.exp(jnp.where(inclusive, differ, 0.0)) * dot_t(queries, keys) * inv_norm(k_row),
        0.0,
    )
    cumul = dot1(upto, jnp.broadcast_to(gate, (TOK, DIM)).astype(BF16))
    solved = solved_ref[...]
    top = dot3(scores[:HALF, :HALF], solved[:HALF])
    bottom = dot3(scores[HALF:, :], solved)
    mixed = jnp.concatenate([top, bottom], axis=0)
    direct_ref[...] = mixed[:, DIM:]
    reach_ref[...] = query_inv * jnp.exp(cumul) * queries.astype(F32) - mixed[:, :DIM]


def first_kernel(own_ref, one_ref, two_ref, three_ref, before_ref, window_ref):
    later = one_ref[...]
    for ref in (two_ref, three_ref):
        step = dot3(later[:, :DIM], ref[...])
        later = jnp.concatenate([step[:, :DIM], step[:, DIM:] + later[:, DIM:]], axis=1)
    before_ref[...] = later
    step = dot3(own_ref[:, :DIM], later)
    window_ref[:, :DIM] = step[:, :DIM]
    window_ref[:, DIM:] = step[:, DIM:] + own_ref[:, DIM:]


def second_kernel(before_ref, window_ref, far_ref, before_out, state_out):
    step = dot3(before_ref[:, :DIM], far_ref[...])
    before_out[:, :DIM] = step[:, :DIM]
    before_out[:, DIM:] = step[:, DIM:] + before_ref[:, DIM:]
    state_out[...] = dot3(window_ref[:, :DIM], far_ref[:, DIM:]) + window_ref[:, DIM:]


def last_kernel(own_ref, before_ref, far_ref, direct_ref, reach_ref, out_ref, state_ref):
    incoming = dot3(before_ref[:, :DIM], far_ref[...]) + before_ref[:, DIM:]
    combined = direct_ref[...] + dot3(reach_ref[...], incoming)
    out_ref[...] = combined.astype(BF16)
    state_ref[...] = dot3(own_ref[:, :DIM], incoming) + own_ref[:, DIM:]


def call(kernel, *shapes):
    def run(*operands):
        vmem = pl.BlockSpec(memory_space=pltpu.VMEM)
        outs = tuple(jax.ShapeDtypeStruct(shape, dtype) for shape, dtype in shapes)
        return pl.pallas_call(
            kernel,
            out_shape=outs,
            in_specs=[vmem] * len(operands),
            out_specs=tuple([vmem] * len(outs)),
            compiler_params=pltpu.CompilerParams(vmem_limit_bytes=48 << 20),
        )(*operands)

    return run


def shifted(block, distance):
    count = lax.axis_size("seq")
    return lax.ppermute(block, "seq", [(i - distance, i) for i in range(distance, count)])


def per_device(query_heads, key_heads, value_heads, gate_log, beta_rate):
    grouping = value_heads.shape[1] // query_heads.shape[1]
    queries = jnp.repeat(jnp.swapaxes(query_heads, 0, 1), grouping, axis=0)
    keys = jnp.repeat(jnp.swapaxes(key_heads, 0, 1), grouping, axis=0)
    values = jnp.swapaxes(value_heads, 0, 1)
    rates = jnp.concatenate([gate_log.T, beta_rate.T], axis=1)[:, None, :]
    rates = jnp.pad(rates, ((0, 0), (0, 7), (0, DIM - 2 * PER)))
    packed = jnp.concatenate([queries, keys, values, rates], axis=1)
    got = lax.all_to_all(packed, "head", split_axis=0, concat_axis=0, tiled=True)
    pair = ((DIM, 2 * DIM), F32)
    own, solved = call(local_kernel, pair, ((TOK, 2 * DIM), F32))(got)
    near = [shifted(own, distance) for distance in (1, 2, 3)]
    direct, reach = call(readout_kernel, ((TOK, DIM), F32), ((TOK, DIM), F32))(got, solved)
    before, window = call(first_kernel, pair, pair)(own, *near)
    before, state = call(second_kernel, pair, ((DIM, DIM), F32))(before, window, shifted(window, 4))
    rows, last_state = call(last_kernel, ((TOK, DIM), BF16), ((DIM, DIM), F32))(
        own, before, shifted(state, 8), direct, reach
    )
    head_output = lax.all_to_all(rows, "head", split_axis=0, concat_axis=1, tiled=True)
    return head_output, last_state[None, None]


def solution(mesh):
    return jax.shard_map(
        per_device,
        mesh=mesh,
        in_specs=(
            P(("seq", "head"), None, None),
            P(("seq", "head"), None, None),
            P(("seq", "head"), None, None),
            P(("seq", "head"), None),
            P(("seq", "head"), None),
        ),
        out_specs=(P(("seq", "head"), None), P("seq", "head", None, None)),
        check_vma=False,
    )
```

time: 272 us -> 93.4 us (0.34)
  waiting for transfers between devices: 125 us -> 13.3 us
  starting transfers between devices: 72.3 us -> 12.2 us
  blocking collectives: 0 us -> 51.5 us
  other arithmetic: 42.1 us -> 0.12 us
  matrix products: 15.5 us -> 0 us
  Pallas kernels: 0 us -> 12.5 us
  local copies, waits for them, and re-layouts: 14.5 us -> 2.57 us
    all_to_all x6 -> x0, waiting for transfers between devices: 57 us -> none  [the longest x1 12.5 us: per_device(): lax.all_to_all(value_heads, 'head', split_axis=1, concat_axis=0, tiled=True)]
    ppermute x15 -> x5, waiting for transfers between devices: 68.3 us -> 13.3 us  [shifted(): lax.ppermute(block, 'seq', [(i - distance, i) for i in range(distance, co...]
    all_to_all x0 -> x2, blocking collectives: none -> 51.5 us  [the longest x1 33.8 us: per_device(): lax.all_to_all(packed, 'head', split_axis=0, concat_axis=0, tiled=True)]
    all_to_all x6 -> x0, starting transfers between devices: 43.5 us -> none  [the longest x1 16 us: per_device(): lax.all_to_all(gate_log, 'head', split_axis=1, concat_axis=0, tiled=True)]
    another operation x3 -> x0, other arithmetic: 39.5 us -> none  [the longest x2 39.3 us: stretch_parts(): jax.scipy.linalg.solve_triangular(identity + lower_triangle, right_side,...]
    ppermute x15 -> x5, starting transfers between devices: 28.8 us -> 12.2 us  [shifted(): lax.ppermute(block, 'seq', [(i - distance, i) for i in range(distance, co...]
    dot_general x35 -> x0, matrix products: 14.9 us -> none  [the longest x29 10.4 us: product(): jnp.einsum('...ij,...jk->...ik', left_mat, right_mat, precision=HIGHEST)]
    pallas_call x0 -> x5, Pallas kernels: none -> 12.5 us  [run(): pl.pallas_call(kernel, out_shape=outs, in_specs=[vmem] * len(operands), o...]
  transfers between devices with their start and end apart: 21 -> 5, of which waited for: 20 -> 4; matrix products, arithmetic and copies ran while one was open for 21% -> 0% of each run, Pallas kernels for 0% -> 2%
where the time goes in v1:
time: 93.4 us; the launch traced here: 93.1 us
  blocking collectives  51.5 us (55%)
  waiting for transfers between devices  13.3 us (14%)
  Pallas kernels  12.5 us (13%)
  starting transfers between devices  12.2 us (13%)
  local copies, waits for them, and re-layouts  2.57 us (3%)
    all_to_all x1, blocking collectives, per_device(): lax.all_to_all(packed, 'head', split_axis=0, concat_axis=0, tiled=True)  33.8 us
    all_to_all x1, blocking collectives, per_device(): lax.all_to_all(rows, 'head', split_axis=0, concat_axis=1, tiled=True)  17.8 us
    ppermute x5, waiting for transfers between devices, shifted(): lax.ppermute(block, 'seq', [(i - distance, i) for i in range(distance, co...  13.3 us
    pallas_call x5, Pallas kernels, run(): pl.pallas_call(kernel, out_shape=outs, in_specs=[vmem] * len(operands), o...  12.5 us
    ppermute x5, starting transfers between devices, shifted(): lax.ppermute(block, 'seq', [(i - distance, i) for i in range(distance, co...  12.2 us
  transfers between devices with their start and end apart: 5, of which 4 were waited for; matrix products, arithmetic and copies ran while one was open for 0% of the time, Pallas kernels for 2%

profile of v1, /device:TPU:4, one launch (start us, length us, event | category | flops | bytes accessed | tf_op | source)
XLA Modules:
  0.0 93.1 jit_solution(7915413549714540154)
XLA Ops:
  0.6 0.0 copy-start.3
  0.6 0.0 copy-start.1
  0.6 0.8 copy.16
  1.5 0.0 copy-done.3
  1.5 0.1 copy.17
  1.5 0.1 maximum_bitcast_fusion
  1.6 0.0 copy-start.2
  1.7 0.0 copy-done.1
  1.7 0.0 copy-start
  1.7 0.8 copy-done.2
  2.5 0.1 copy-done
  2.6 0.1 copy.23
  2.7 33.8 %all_to_all.24.got_ref = bf16[32,56,128]{2,1,0:T(8,128)(2,1)S(1)} all-to-all(bf16[32,56,128]{2,1,0:T(8,128)(2,1)S(1)} %fusion.1), channel_id=1, replica_groups=mesh['seq'=16,'head'=32] {'head'}, dimensions={0} | all-to-all | bytes 917504 | tf_op jit(solution)/shard_map/all_to_all | solution.py:204
  36.5 9.0 %shard_map.68 = (f32[128,256]{1,0:T(8,128)S(1)}, f32[512,256]{1,0:T(8,128)S(1)}) custom-call(bf16[32,56,128]{2,1,0:T(8,128)(2,1)S(1)} %all_to_all.24.got_ref), custom_call_target="tpu_custom_call" | custom-call | tf_op jit(solution)/shard_map/pallas_call | solution.py:180
  45.5 1.9 %collective-permute-start.2 = (f32[128,256]{1,0:T(8,128)S(1)}, f32[128,256]{1,0:T(8,128)S(1)}, u32[]{:S(2)}, u32[]{:S(2)}) collective-permute-start(f32[128,256]{1,0:T(8,128)S(1)} %get-tuple-element.12.own_ref), channel_id=1, source_target_pairs={{0,96},{32,128},{64,160},{96,192},{128,224},{160,256},{192,288},{2... | collective-permute-start | bytes 393224 | tf_op jit(solution)/shard_map/ppermute | solution.py:193
  47.4 3.6 %collective-permute-start.1 = (f32[128,256]{1,0:T(8,128)S(1)}, f32[128,256]{1,0:T(8,128)S(1)}, u32[]{:S(2)}, u32[]{:S(2)}) collective-permute-start(f32[128,256]{1,0:T(8,128)S(1)} %get-tuple-element.12.own_ref), channel_id=1, source_target_pairs={{0,64},{32,96},{64,128},{96,160},{128,192},{160,224},{192,256},{22... | collective-permute-start | bytes 393224 | tf_op jit(solution)/shard_map/ppermute | solution.py:193
  51.0 2.9 %collective-permute-start = (f32[128,256]{1,0:T(8,128)S(1)}, f32[128,256]{1,0:T(8,128)S(1)}, u32[]{:S(2)}, u32[]{:S(2)}) collective-permute-start(f32[128,256]{1,0:T(8,128)S(1)} %get-tuple-element.12.own_ref), channel_id=1, source_target_pairs={{0,32},{32,64},{64,96},{96,128},{128,160},{160,192},{192,224},{224... | collective-permute-start | bytes 393224 | tf_op jit(solution)/shard_map/ppermute | solution.py:193
  54.0 0.0 collective-permute-done.2.three_ref
  54.0 2.4 %collective-permute-done.1.two_ref = f32[128,256]{1,0:T(8,128)S(1)} collective-permute-done((f32[128,256]{1,0:T(8,128)S(1)}, f32[128,256]{1,0:T(8,128)S(1)}, u32[]{:S(2)}, u32[]{:S(2)}) %collective-permute-start.1) | collective-permute-done | bytes 131104 | tf_op jit(solution)/shard_map/ppermute | solution.py:193
  56.3 1.9 %collective-permute-done.one_ref = f32[128,256]{1,0:T(8,128)S(1)} collective-permute-done((f32[128,256]{1,0:T(8,128)S(1)}, f32[128,256]{1,0:T(8,128)S(1)}, u32[]{:S(2)}, u32[]{:S(2)}) %collective-permute-start) | collective-permute-done | bytes 131104 | tf_op jit(solution)/shard_map/ppermute | solution.py:193
  58.2 0.6 shard_map.69
  58.8 2.5 %collective-permute-start.3 = (f32[128,256]{1,0:T(8,128)S(1)}, f32[128,256]{1,0:T(8,128)S(1)}, u32[]{:S(2)}, u32[]{:S(2)}) collective-permute-start(f32[128,256]{1,0:T(8,128)S(1)} %get-tuple-element.14.window_ref), channel_id=1, source_target_pairs={{0,128},{32,160},{64,192},{96,224},{128,256},{160,288},{192,320},{... | collective-permute-start | bytes 393224 | tf_op jit(solution)/shard_map/ppermute | solution.py:193
  61.4 4.3 %collective-permute-done.3.far_ref = f32[128,256]{1,0:T(8,128)S(1)} collective-permute-done((f32[128,256]{1,0:T(8,128)S(1)}, f32[128,256]{1,0:T(8,128)S(1)}, u32[]{:S(2)}, u32[]{:S(2)}) %collective-permute-start.3) | collective-permute-done | bytes 131104 | tf_op jit(solution)/shard_map/ppermute | solution.py:193
  65.7 0.2 shard_map.70
  65.9 1.3 %collective-permute-start.4 = (f32[128,128]{1,0:T(8,128)S(1)}, f32[128,128]{1,0:T(8,128)S(1)}, u32[]{:S(2)}, u32[]{:S(2)}) collective-permute-start(f32[128,128]{1,0:T(8,128)S(1)} %get-tuple-element.16), channel_id=1, source_target_pairs={{0,256},{32,288},{64,320},{96,352},{128,384},{160,416},{192,448},{... | collective-permute-start | bytes 196616 | tf_op jit(solution)/shard_map/ppermute | solution.py:193
  67.2 1.6 %shard_map.71 = (f32[512,128]{1,0:T(8,128)S(1)}, f32[512,128]{1,0:T(8,128)S(1)}) custom-call(bf16[32,56,128]{2,1,0:T(8,128)(2,1)S(1)} %all_to_all.24.got_ref, f32[512,256]{1,0:T(8,128)S(1)} %get-tuple-element.17.solved_ref), custom_call_target="tpu_custom_call" | custom-call | tf_op jit(solution)/shard_map/pallas_call | solution.py:180
  68.8 4.7 %collective-permute-done.4.far_ref = f32[128,128]{1,0:T(8,128)S(1)} collective-permute-done((f32[128,128]{1,0:T(8,128)S(1)}, f32[128,128]{1,0:T(8,128)S(1)}, u32[]{:S(2)}, u32[]{:S(2)}) %collective-permute-start.4) | collective-permute-done | bytes 65568 | tf_op jit(solution)/shard_map/ppermute | solution.py:193
  73.6 1.1 %shard_map.72 = (bf16[512,128]{1,0:T(8,128)(2,1)S(1)}, f32[128,128]{1,0:T(8,128)}) custom-call(f32[128,256]{1,0:T(8,128)S(1)} %get-tuple-element.12.own_ref, f32[128,256]{1,0:T(8,128)S(1)} %get-tuple-element.15.before_ref, f32[128,128]{1,0:T(8,128)S(1)} %collective-permute-done.4.far_ref, f32[512,128]{1,0:T(8,128)S(1)} %get-tuple-element.18.direct_ref, ...), custom_call_target="tpu_custom_call" | custom-call | tf_op jit(solution)/shard_map/pallas_call | solution.py:180
  74.6 17.8 %all_to_all.25 = bf16[32,16,128]{2,1,0:T(8,128)(2,1)S(1)} all-to-all(bf16[32,16,128]{2,1,0:T(8,128)(2,1)S(1)} %bitcast.19), channel_id=1, replica_groups=mesh['seq'=16,'head'=32] {'head'}, dimensions={0} | all-to-all | bytes 262144 | tf_op jit(solution)/shard_map/all_to_all | solution.py:214
  92.4 0.7 copy_bitcast_fusion
  (6 shorter events, 0.1 us)
Async XLA Ops:
  0.6 0.8 copy-start.3
  0.6 1.0 %copy-start.1 = (bf16[16,16,128]{2,1,0:T(8,128)(2,1)S(1)}, bf16[16,16,128]{2,1,0:T(8,128)(2,1)}, u32[]{:S(2)}) copy-start(bf16[16,16,128]{2,1,0:T(8,128)(2,1)} %param.5) | copy-start | bytes 196612
  1.6 0.8 copy-start.2
  1.7 0.9 copy-start
  45.5 8.4 %collective-permute-start.2 = (f32[128,256]{1,0:T(8,128)S(1)}, f32[128,256]{1,0:T(8,128)S(1)}, u32[]{:S(2)}, u32[]{:S(2)}) collective-permute-start(f32[128,256]{1,0:T(8,128)S(1)} %get-tuple-element.12.own_ref), channel_id=1, source_target_pairs={{0,96},{32,128},{64,160},{96,192},{128,224},{160,256},{192,288},{2... | collective-permute-start | bytes 393224 | tf_op jit(solution)/shard_map/ppermute | solution.py:193
  47.4 8.9 %collective-permute-start.1 = (f32[128,256]{1,0:T(8,128)S(1)}, f32[128,256]{1,0:T(8,128)S(1)}, u32[]{:S(2)}, u32[]{:S(2)}) collective-permute-start(f32[128,256]{1,0:T(8,128)S(1)} %get-tuple-element.12.own_ref), channel_id=1, source_target_pairs={{0,64},{32,96},{64,128},{96,160},{128,192},{160,224},{192,256},{22... | collective-permute-start | bytes 393224 | tf_op jit(solution)/shard_map/ppermute | solution.py:193
  51.0 7.2 %collective-permute-start = (f32[128,256]{1,0:T(8,128)S(1)}, f32[128,256]{1,0:T(8,128)S(1)}, u32[]{:S(2)}, u32[]{:S(2)}) collective-permute-start(f32[128,256]{1,0:T(8,128)S(1)} %get-tuple-element.12.own_ref), channel_id=1, source_target_pairs={{0,32},{32,64},{64,96},{96,128},{128,160},{160,192},{192,224},{224... | collective-permute-start | bytes 393224 | tf_op jit(solution)/shard_map/ppermute | solution.py:193
  58.8 6.9 %collective-permute-start.3 = (f32[128,256]{1,0:T(8,128)S(1)}, f32[128,256]{1,0:T(8,128)S(1)}, u32[]{:S(2)}, u32[]{:S(2)}) collective-permute-start(f32[128,256]{1,0:T(8,128)S(1)} %get-tuple-element.14.window_ref), channel_id=1, source_target_pairs={{0,128},{32,160},{64,192},{96,224},{128,256},{160,288},{192,320},{... | collective-permute-start | bytes 393224 | tf_op jit(solution)/shard_map/ppermute | solution.py:193
  65.9 7.7 %collective-permute-start.4 = (f32[128,128]{1,0:T(8,128)S(1)}, f32[128,128]{1,0:T(8,128)S(1)}, u32[]{:S(2)}, u32[]{:S(2)}) collective-permute-start(f32[128,128]{1,0:T(8,128)S(1)} %get-tuple-element.16), channel_id=1, source_target_pairs={{0,256},{32,288},{64,320},{96,352},{128,384},{160,416},{192,448},{... | collective-permute-start | bytes 196616 | tf_op jit(solution)/shard_map/ppermute | solution.py:193

commit v2 on v1

v2 whole, which is shorter than its diff:
```python
import jax
import jax.numpy as jnp
from jax import lax
from jax.experimental import pallas as pl
from jax.experimental.pallas import tpu as pltpu
from jax.sharding import PartitionSpec as P

F32 = jnp.float32
BF16 = jnp.bfloat16
TOK = 512
DIM = 128
SRC = 32
PER = 16
HALF = 256


def iota(shape, dim):
    return lax.broadcasted_iota(jnp.int32, shape, dim)


def dot1(a, b):
    return lax.dot_general(a, b, (((1,), (0,)), ((), ())), preferred_element_type=F32)


def dot_t(a, b):
    return lax.dot_general(a, b, (((1,), (1,)), ((), ())), preferred_element_type=F32)


def split(a):
    high = a.astype(BF16)
    return high, (a - high.astype(F32)).astype(BF16)


def dot3(a, b):
    ah, al = split(a)
    bh, bl = split(b)
    return dot1(ah, bh) + (dot1(ah, bl) + dot1(al, bh))


def inv_norm(total):
    total = total + 1e-6
    y = lax.rsqrt(total)
    return y * (1.5 - 0.5 * total * y * y)


def row_sums(x):
    squares = x.astype(F32) * x.astype(F32)
    column = jnp.sum(squares, axis=1, keepdims=True)
    high, low = split(squares)
    ones = jnp.ones((8, DIM), BF16)
    row = (dot_t(ones, high) + dot_t(ones, low))[0:1]
    return column, row


def dot_pair(a, b):
    ah, al = split(a)
    bh, bl = split(b)
    return dot1(jnp.concatenate([ah, al], axis=1), jnp.concatenate([bh, bh], axis=0)) + dot1(ah, bl)


def columns_of(got_ref):
    lanes = got_ref[:, 48:56, :].astype(F32)[:, 0, :].astype(BF16)
    token, source = iota((TOK, SRC), 0), iota((TOK, SRC), 1)
    spread = ((token >> 4) == source).astype(F32).astype(BF16)
    rows = dot1(spread, lanes)
    lane = iota((TOK, DIM), 1)
    spot = iota((TOK, DIM), 0) & (PER - 1)
    gate = jnp.sum(jnp.where(lane == spot, rows, 0.0), axis=1, keepdims=True)
    beta = jnp.sum(jnp.where(lane == spot + PER, rows, 0.0), axis=1, keepdims=True)
    return gate, beta


def spans(gate):
    row, col = iota((HALF, HALF), 0), iota((HALF, HALF), 1)
    upto = (row >= col).astype(F32).astype(BF16)
    first, second = gate[:HALF], gate[HALF:]
    after1 = jnp.where(row > col, first, 0.0).astype(BF16)
    after2 = jnp.where(row > col, second, 0.0).astype(BF16)
    wide = jnp.broadcast_to(second, (HALF, HALF)).astype(BF16)
    whole = dot1(
        jnp.concatenate([jnp.ones((HALF, HALF), BF16), upto], axis=1),
        jnp.concatenate([after1, wide], axis=0),
    )
    return dot1(upto, after1), whole, dot1(upto, after2), row, col


def local_kernel(got_ref, pair_ref, solved_ref):
    gate, beta = columns_of(got_ref)
    keys = got_ref[:, 16:32, :].reshape(TOK, DIM)
    values = got_ref[:, 32:48, :].reshape(TOK, DIM)
    d11, d21, d22, row, col = spans(gate)
    k_col, k_row = row_sums(keys)
    inv_col, inv_row = inv_norm(k_col), inv_norm(k_row)
    strict = row > col
    scale = beta * inv_col
    k1, k2 = keys[:HALF], keys[HALF:]
    l11 = jnp.where(strict, scale[:HALF] * jnp.exp(jnp.where(strict, d11, 0.0)) * dot_t(k1, k1) * inv_row[:, :HALF], 0.0)
    l22 = jnp.where(strict, scale[HALF:] * jnp.exp(jnp.where(strict, d22, 0.0)) * dot_t(k2, k2) * inv_row[:, HALF:], 0.0)
    l21 = scale[HALF:] * jnp.exp(d21) * dot_t(k2, k1) * inv_row[:, :HALF]
    cumul = jnp.concatenate([d11[:, :1], d21[:, :1]], axis=0) + gate[:1]
    gate_wide = jnp.broadcast_to(gate, (TOK, DIM)).astype(BF16)
    later = (row < col).astype(F32).astype(BF16)
    beyond = jnp.concatenate(
        [
            dot1(jnp.concatenate([later, jnp.ones((HALF, HALF), BF16)], axis=1), gate_wide),
            dot1(later, gate_wide[HALF:]),
        ],
        axis=0,
    )
    right = jnp.concatenate(
        [(scale * jnp.exp(cumul)) * keys.astype(F32), beta * values.astype(F32)], axis=1
    )
    apart = iota((DIM, DIM), 0) ^ iota((DIM, DIM), 1)
    eye = jnp.where(apart == 0, 1.0, 0.0)
    blocks = [l11[:DIM, :DIM], l11[DIM:, DIM:], l22[:DIM, :DIM], l22[DIM:, DIM:]]
    n1 = [jnp.where(apart < 16, -b, 0.0) for b in blocks]
    n2 = [dot_pair(n, n) for n in n1]
    x = [eye + n + m + dot_pair(n, m) for n, m in zip(n1, n2)]
    n4 = [dot_pair(n, n) for n in n2]
    x = [y + dot_pair(y, n) for y, n in zip(x, n4)]
    n8 = [dot_pair(n, n) for n in n4]
    x = [y + dot_pair(y, n) for y, n in zip(x, n8)]
    for width in (16, 32, 64):
        here = (apart >= width) & (apart < 2 * width)
        half = [dot_pair(jnp.where(here, b, 0.0), y) for b, y in zip(blocks, x)]
        x = [y - dot_pair(y, z) for y, z in zip(x, half)]
    merged = []
    for lo, hi, tie in ((x[0], x[1], l11[DIM:, :DIM]), (x[2], x[3], l22[DIM:, :DIM])):
        cross = -dot_pair(hi, dot_pair(tie, lo))
        merged.append(
            jnp.concatenate(
                [jnp.concatenate([lo, jnp.zeros_like(lo)], axis=1), jnp.concatenate([cross, hi], axis=1)], axis=0
            )
        )
    top = dot3(merged[0], right[:HALF])
    parts = [top, dot3(merged[1], right[HALF:] - dot3(l21, top))]
    solved = jnp.concatenate(parts, axis=0)
    solved_ref[...] = solved
    weight = inv_col * jnp.exp(beyond)
    scaled = jnp.concatenate([weight, weight], axis=1) * solved
    high, low = split(scaled)
    keys_t = keys.T
    moved = dot1(keys_t, high) + dot1(keys_t, low)
    carry = jnp.where(apart == 0, jnp.exp(cumul[TOK - 1 :]), 0.0)
    pair_ref[:, :DIM] = carry - moved[:, :DIM]
    pair_ref[:, DIM:] = moved[:, DIM:]


def readout_kernel(got_ref, solved_ref, before_ref, direct_ref, reach_ref):
    gate, _ = columns_of(got_ref)
    queries = got_ref[:, 0:16, :].reshape(TOK, DIM)
    keys = got_ref[:, 16:32, :].reshape(TOK, DIM)
    d11, d21, d22, row, col = spans(gate)
    q_col, _ = row_sums(queries)
    _, k_row = row_sums(keys)
    query_inv, key_inv = inv_norm(q_col), inv_norm(k_row)
    inclusive = row >= col
    q1, q2, k1, k2 = queries[:HALF], queries[HALF:], keys[:HALF], keys[HALF:]
    i1, i2 = query_inv[:HALF], query_inv[HALF:]
    s11 = jnp.where(inclusive, i1 * jnp.exp(jnp.where(inclusive, d11, 0.0)) * dot_t(q1, k1) * key_inv[:, :HALF], 0.0)
    s22 = jnp.where(inclusive, i2 * jnp.exp(jnp.where(inclusive, d22, 0.0)) * dot_t(q2, k2) * key_inv[:, HALF:], 0.0)
    s21 = i2 * jnp.exp(d21) * dot_t(q2, k1) * key_inv[:, :HALF]
    cumul = jnp.concatenate([d11[:, :1], d21[:, :1]], axis=0) + gate[:1]
    solved = solved_ref[...]
    top = dot3(s11, solved[:HALF])
    bottom = dot3(jnp.concatenate([s21, s22], axis=1), solved)
    mixed = jnp.concatenate([top, bottom], axis=0)
    reach = query_inv * jnp.exp(cumul) * queries.astype(F32) - mixed[:, :DIM]
    step = dot3(reach, before_ref[...])
    reach_ref[...] = step[:, :DIM]
    direct_ref[...] = mixed[:, DIM:] + step[:, DIM:]


def after(later, earlier):
    step = dot3(later[:, :DIM], earlier)
    return jnp.concatenate([step[:, :DIM], step[:, DIM:] + later[:, DIM:]], axis=1)


def group_kernel(spot_ref, group_ref, before_ref, upto_ref, total_ref):
    spot = spot_ref[0]
    d_row, d_col = iota((DIM, 2 * DIM), 0), iota((DIM, 2 * DIM), 1)
    chain = [jnp.where(d_row == d_col, 1.0, 0.0), group_ref[0]]
    for step in range(1, 4):
        chain.append(after(group_ref[step], chain[-1]))
    before, upto = chain[0], chain[1]
    for step in range(1, 4):
        before = jnp.where(spot == step, chain[step], before)
        upto = jnp.where(spot == step, chain[step + 1], upto)
    before_ref[...] = before
    upto_ref[...] = upto
    total_ref[...] = chain[4]


def last_kernel(one_ref, two_ref, three_ref, upto_ref, direct_ref, reach_ref, out_ref, state_ref):
    arriving = dot3(two_ref[:, :DIM], three_ref[...]) + two_ref[:, DIM:]
    arriving = dot3(one_ref[:, :DIM], arriving) + one_ref[:, DIM:]
    out_ref[...] = (direct_ref[...] + dot3(reach_ref[...], arriving)).astype(BF16)
    state_ref[...] = dot3(upto_ref[:, :DIM], arriving) + upto_ref[:, DIM:]


def call(kernel, *shapes):
    def run(*operands):
        vmem = pl.BlockSpec(memory_space=pltpu.VMEM)
        outs = tuple(jax.ShapeDtypeStruct(shape, dtype) for shape, dtype in shapes)
        return pl.pallas_call(
            kernel,
            out_shape=outs,
            in_specs=[
                pl.BlockSpec(memory_space=pltpu.SMEM) if x.dtype == jnp.int32 else vmem for x in operands
            ],
            out_specs=tuple([vmem] * len(outs)),
            compiler_params=pltpu.CompilerParams(vmem_limit_bytes=48 << 20),
        )(*operands)

    return run


def shifted(block, distance):
    count = lax.axis_size("seq")
    return lax.ppermute(block, "seq", [(i - distance, i) for i in range(distance, count)])


def per_device(query_heads, key_heads, value_heads, gate_log, beta_rate):
    grouping = value_heads.shape[1] // query_heads.shape[1]
    queries = jnp.repeat(jnp.swapaxes(query_heads, 0, 1), grouping, axis=0)
    keys = jnp.repeat(jnp.swapaxes(key_heads, 0, 1), grouping, axis=0)
    values = jnp.swapaxes(value_heads, 0, 1)
    rates = jnp.concatenate([gate_log.T, beta_rate.T], axis=1)[:, None, :]
    rates = jnp.pad(rates, ((0, 0), (0, 7), (0, DIM - 2 * PER)))
    packed = jnp.concatenate([queries, keys, values, rates], axis=1)
    got = lax.all_to_all(packed, "head", split_axis=0, concat_axis=0, tiled=True)
    pair = ((DIM, 2 * DIM), F32)
    own, solved = call(local_kernel, pair, ((TOK, 2 * DIM), F32))(got)
    count = lax.axis_size("seq")
    groups = [list(range(first, first + 4)) for first in range(0, count, 4)]
    group = lax.all_gather(own, "seq", axis_index_groups=groups)
    spot = (lax.axis_index("seq") % 4).astype(jnp.int32)[None]
    before, upto, total = call(group_kernel, pair, pair, pair)(spot, group)
    one, two, three = shifted(total, 4), shifted(total, 8), shifted(total[:, DIM:], 12)
    direct, reach = call(readout_kernel, ((TOK, DIM), F32), ((TOK, DIM), F32))(got, solved, before)
    rows, last_state = call(last_kernel, ((TOK, DIM), BF16), ((DIM, DIM), F32))(
        one, two, three, upto, direct, reach
    )
    head_output = lax.all_to_all(rows, "head", split_axis=0, concat_axis=1, tiled=True)
    return head_output, last_state[None, None]


def solution(mesh):
    return jax.shard_map(
        per_device,
        mesh=mesh,
        in_specs=(
            P(("seq", "head"), None, None),
            P(("seq", "head"), None, None),
            P(("seq", "head"), None, None),
            P(("seq", "head"), None),
            P(("seq", "head"), None),
        ),
        out_specs=(P(("seq", "head"), None), P("seq", "head", None, None)),
        check_vma=False,
    )
```

time: 93.4 us -> 81.5 us (0.87)
  blocking collectives: 51.5 us -> 25 us
  waiting for transfers between devices: 13.3 us -> 23.2 us
  starting transfers between devices: 12.2 us -> 21 us
  Pallas kernels: 12.5 us -> 7.67 us
    all_to_all x1 -> x0, blocking collectives: 33.8 us -> none  [per_device(): lax.all_to_all(packed, 'head', split_axis=0, concat_axis=0, tiled=True)]
    all_to_all x0 -> x1, waiting for transfers between devices: none -> 18 us  [per_device(): lax.all_to_all(packed, 'head', split_axis=0, concat_axis=0, tiled=True)]
    all_to_all x0 -> x1, starting transfers between devices: none -> 16 us  [per_device(): lax.all_to_all(packed, 'head', split_axis=0, concat_axis=0, tiled=True)]
    ppermute x5 -> x3, waiting for transfers between devices: 13.3 us -> 5.24 us  [shifted(): lax.ppermute(block, 'seq', [(i - distance, i) for i in range(distance, co...]
    all_gather x0 -> x1, blocking collectives: none -> 7.33 us  [per_device(): group = lax.all_gather(own, 'seq', axis_index_groups=groups)]
    ppermute x5 -> x3, starting transfers between devices: 12.2 us -> 5.06 us  [shifted(): lax.ppermute(block, 'seq', [(i - distance, i) for i in range(distance, co...]
    pallas_call x5 -> x4, Pallas kernels: 12.5 us -> 7.67 us  [run(): pl.pallas_call(kernel, out_shape=outs, in_specs=[pl.BlockSpec(memory_spac...]
  transfers between devices with their start and end apart: 5 -> 4, of which waited for: 4 -> 3; matrix products, arithmetic and copies ran while one was open for 0% -> 0% of each run, Pallas kernels for 2% -> 2%
where the time goes in v2:
time: 81.5 us; the launch traced here: 81.2 us
  blocking collectives  25 us (31%)
  waiting for transfers between devices  23.2 us (28%)
  starting transfers between devices  21 us (26%)
  Pallas kernels  7.67 us (9%)
  local copies, waits for them, and re-layouts  2.58 us (3%)
  other arithmetic  0.91 us (1%)
    all_to_all x1, waiting for transfers between devices, per_device(): lax.all_to_all(packed, 'head', split_axis=0, concat_axis=0, tiled=True)  18 us
    all_to_all x1, blocking collectives, per_device(): lax.all_to_all(rows, 'head', split_axis=0, concat_axis=1, tiled=True)  17.6 us
    all_to_all x1, starting transfers between devices, per_device(): lax.all_to_all(packed, 'head', split_axis=0, concat_axis=0, tiled=True)  16 us
    pallas_call x4, Pallas kernels, run(): pl.pallas_call(kernel, out_shape=outs, in_specs=[pl.BlockSpec(memory_spac...  7.67 us
    all_gather x1, blocking collectives, per_device(): group = lax.all_gather(own, 'seq', axis_index_groups=groups)  7.33 us
    ppermute x3, waiting for transfers between devices, shifted(): lax.ppermute(block, 'seq', [(i - distance, i) for i in range(distance, co...  5.24 us
    ppermute x3, starting transfers between devices, shifted(): lax.ppermute(block, 'seq', [(i - distance, i) for i in range(distance, co...  5.06 us
    unnamed x11, local copies, waits for them, and re-layouts  1.81 us
  transfers between devices with their start and end apart: 4, of which 3 were waited for; matrix products, arithmetic and copies ran while one was open for 0% of the time, Pallas kernels for 2%

profile of v2, /device:TPU:4, one launch (start us, length us, event | category | flops | bytes accessed | tf_op | source)
XLA Modules:
  0.0 81.2 jit_solution(18378647374871147731)
XLA Ops:
  0.6 0.0 copy-start.3
  0.6 0.0 copy-start.1
  0.6 0.8 copy.16
  1.5 0.0 copy-done.3
  1.5 0.1 copy.17
  1.5 0.1 maximum_bitcast_fusion
  1.6 0.0 copy-start.2
  1.7 0.0 copy-done.1
  1.7 0.0 copy-start
  1.7 0.8 copy-done.2
  2.5 0.1 copy-done
  2.6 0.1 copy.23
  2.7 0.8 %fusion.1 = bf16[32,56,128]{2,1,0:T(8,128)(2,1)} fusion(bf16[32,1,32]{2,1,0:T(2,128)(2,1)S(1)} %copy.18, bf16[32,16,128]{2,1,0:T(8,128)(2,1)S(1)} %bitcast.23, bf16[32,16,128]{2,1,0:T(8,128)(2,1)S(1)} %bitcast.25, bf16[32,16,128]{2,1,0:T(8,128)(2,1)S(1)} %bitcast.24), kind=kLoop, calls=%fused_computation.2 | loop fusion | flops 2293760 | bytes 854016 | tf_op jit(solution)/shard_map/concatenate | solution.py:230
  3.5 16.0 %all-to-all-start = ((bf16[32,56,128]{2,1,0:T(8,128)(2,1)}), bf16[32,56,128]{2,1,0:T(8,128)(2,1)S(1)}, u32[]{:S(2)}, u32[]{:S(2)}) async-start(bf16[32,56,128]{2,1,0:T(8,128)(2,1)} %fusion.1), calls=%async_computation | async-start | bytes 917504 | tf_op jit(solution)/shard_map/all_to_all | solution.py:231
  19.5 18.0 %all-to-all-done.got_ref = bf16[32,56,128]{2,1,0:T(8,128)(2,1)S(1)} async-done(((bf16[32,56,128]{2,1,0:T(8,128)(2,1)}), bf16[32,56,128]{2,1,0:T(8,128)(2,1)S(1)}, u32[]{:S(2)}, u32[]{:S(2)}) %all-to-all-start) | async-done | bytes 458784 | tf_op jit(solution)/shard_map/all_to_all | solution.py:231
  37.5 4.2 %shard_map.68 = (f32[128,256]{1,0:T(8,128)S(1)}, f32[512,256]{1,0:T(8,128)S(1)}) custom-call(bf16[32,56,128]{2,1,0:T(8,128)(2,1)S(1)} %all-to-all-done.got_ref), custom_call_target="tpu_custom_call" | custom-call | tf_op jit(solution)/shard_map/pallas_call | solution.py:205
  41.7 7.3 %all-gather = f32[512,256]{1,0:T(8,128)S(1)} all-gather(f32[128,256]{1,0:T(8,128)S(1)} %get-tuple-element.11), channel_id=2, replica_groups={{0,32,64,96},{128,160,192,224},{256,288,320,352},{384,416,448,480},{1,3..., dimensions={0}, use_global_device_ids=true | all-gather | bytes 655360 | tf_op jit(solution)/shard_map/all_gather | solution.py:236
  49.0 0.6 shard_map.69
  49.7 1.3 %collective-permute-start.1 = (f32[128,256]{1,0:T(8,128)S(1)}, f32[128,256]{1,0:T(8,128)S(1)}, u32[]{:S(2)}, u32[]{:S(2)}) collective-permute-start(f32[128,256]{1,0:T(8,128)S(1)} %get-tuple-element.12), channel_id=1, source_target_pairs={{0,256},{32,288},{64,320},{96,352},{128,384},{160,416},{192,448},{... | collective-permute-start | bytes 393224 | tf_op jit(solution)/shard_map/ppermute | solution.py:220
  51.0 3.1 %collective-permute-start = (f32[128,256]{1,0:T(8,128)S(1)}, f32[128,256]{1,0:T(8,128)S(1)}, u32[]{:S(2)}, u32[]{:S(2)}) collective-permute-start(f32[128,256]{1,0:T(8,128)S(1)} %get-tuple-element.12), channel_id=1, source_target_pairs={{0,128},{32,160},{64,192},{96,224},{128,256},{160,288},{192,320},{... | collective-permute-start | bytes 393224 | tf_op jit(solution)/shard_map/ppermute | solution.py:220
  54.1 0.7 collective-permute-start.2
  54.8 1.6 %shard_map.70 = (f32[512,128]{1,0:T(8,128)S(1)}, f32[512,128]{1,0:T(8,128)S(1)}) custom-call(bf16[32,56,128]{2,1,0:T(8,128)(2,1)S(1)} %all-to-all-done.got_ref, f32[512,256]{1,0:T(8,128)S(1)} %get-tuple-element.14.solved_ref, f32[128,256]{1,0:T(8,128)S(1)} %get-tuple-element.15.before_ref), custom_call_target="tpu_custom_call" | custom-call | tf_op jit(solution)/shard_map/pallas_call | solution.py:205
  56.4 0.0 collective-permute-done.2.three_ref
  56.4 3.0 %collective-permute-done.1.two_ref = f32[128,256]{1,0:T(8,128)S(1)} collective-permute-done((f32[128,256]{1,0:T(8,128)S(1)}, f32[128,256]{1,0:T(8,128)S(1)}, u32[]{:S(2)}, u32[]{:S(2)}) %collective-permute-start.1) | collective-permute-done | bytes 131104 | tf_op jit(solution)/shard_map/ppermute | solution.py:220
  59.4 2.2 %collective-permute-done.one_ref = f32[128,256]{1,0:T(8,128)S(1)} collective-permute-done((f32[128,256]{1,0:T(8,128)S(1)}, f32[128,256]{1,0:T(8,128)S(1)}, u32[]{:S(2)}, u32[]{:S(2)}) %collective-permute-start) | collective-permute-done | bytes 131104 | tf_op jit(solution)/shard_map/ppermute | solution.py:220
  61.6 1.2 %shard_map.71 = (bf16[512,128]{1,0:T(8,128)(2,1)S(1)}, f32[128,128]{1,0:T(8,128)}) custom-call(f32[128,256]{1,0:T(8,128)S(1)} %collective-permute-done.one_ref, f32[128,256]{1,0:T(8,128)S(1)} %collective-permute-done.1.two_ref, f32[128,128]{1,0:T(8,128)S(1)} %collective-permute-done.2.three_ref, f32[128,256]{1,0:T(8,128)S(1)} %get-tuple-element.13.upto_ref, ...), custom_call_target="tpu_custom_call" | custom-call | tf_op jit(solution)/shard_map/pallas_call | solution.py:205
  62.9 17.6 %all_to_all.24 = bf16[32,16,128]{2,1,0:T(8,128)(2,1)S(1)} all-to-all(bf16[32,16,128]{2,1,0:T(8,128)(2,1)S(1)} %bitcast.22), channel_id=1, replica_groups=mesh['seq'=16,'head'=32] {'head'}, dimensions={0} | all-to-all | bytes 262144 | tf_op jit(solution)/shard_map/all_to_all | solution.py:244
  80.5 0.7 copy_bitcast_fusion
  (6 shorter events, 0.1 us)
Async XLA Ops:
  0.6 0.8 %copy-start.3 = (bf16[16,32]{1,0:T(8,128)(2,1)S(1)}, bf16[16,32]{1,0:T(8,128)(2,1)}, u32[]{:S(2)}) copy-start(bf16[16,32]{1,0:T(8,128)(2,1)} %param.9) | copy-start | bytes 3076
  0.6 1.0 %copy-start.1 = (bf16[16,16,128]{2,1,0:T(8,128)(2,1)S(1)}, bf16[16,16,128]{2,1,0:T(8,128)(2,1)}, u32[]{:S(2)}) copy-start(bf16[16,16,128]{2,1,0:T(8,128)(2,1)} %param.5) | copy-start | bytes 196612
  1.6 0.8 %copy-start.2 = (bf16[16,16,128]{2,1,0:T(8,128)(2,1)S(1)}, bf16[16,16,128]{2,1,0:T(8,128)(2,1)}, u32[]{:S(2)}) copy-start(bf16[16,16,128]{2,1,0:T(8,128)(2,1)} %param.6) | copy-start | bytes 196612
  1.7 0.9 %copy-start = (bf16[16,32,128]{2,1,0:T(8,128)(2,1)S(1)}, bf16[16,32,128]{2,1,0:T(8,128)(2,1)}, u32[]{:S(2)}) copy-start(bf16[16,32,128]{2,1,0:T(8,128)(2,1)} %param.7) | copy-start | bytes 393220
  3.5 34.0 %all-to-all-start = ((bf16[32,56,128]{2,1,0:T(8,128)(2,1)}), bf16[32,56,128]{2,1,0:T(8,128)(2,1)S(1)}, u32[]{:S(2)}, u32[]{:S(2)}) async-start(bf16[32,56,128]{2,1,0:T(8,128)(2,1)} %fusion.1), calls=%async_computation | async-start | bytes 917504 | tf_op jit(solution)/shard_map/all_to_all | solution.py:231
  49.7 9.7 %collective-permute-start.1 = (f32[128,256]{1,0:T(8,128)S(1)}, f32[128,256]{1,0:T(8,128)S(1)}, u32[]{:S(2)}, u32[]{:S(2)}) collective-permute-start(f32[128,256]{1,0:T(8,128)S(1)} %get-tuple-element.12), channel_id=1, source_target_pairs={{0,256},{32,288},{64,320},{96,352},{128,384},{160,416},{192,448},{... | collective-permute-start | bytes 393224 | tf_op jit(solution)/shard_map/ppermute | solution.py:220
  51.0 10.7 %collective-permute-start = (f32[128,256]{1,0:T(8,128)S(1)}, f32[128,256]{1,0:T(8,128)S(1)}, u32[]{:S(2)}, u32[]{:S(2)}) collective-permute-start(f32[128,256]{1,0:T(8,128)S(1)} %get-tuple-element.12), channel_id=1, source_target_pairs={{0,128},{32,160},{64,192},{96,224},{128,256},{160,288},{192,320},{... | collective-permute-start | bytes 393224 | tf_op jit(solution)/shard_map/ppermute | solution.py:220
  54.1 2.3 %collective-permute-start.2 = (f32[128,128]{1,0:T(8,128)S(1)}, f32[128,128]{1,0:T(8,128)S(1)}, u32[]{:S(2)}, u32[]{:S(2)}) collective-permute-start(f32[128,128]{1,0:T(8,128)S(1)} %slice.3), channel_id=1, source_target_pairs={{0,384},{32,416},{64,448},{96,480},{1,385},{33,417},{65,449},{97,4... | collective-permute-start | bytes 196616 | tf_op jit(solution)/shard_map/ppermute | solution.py:220

commit v3 on v2

--- a/solution.py
+++ b/solution.py
@@ -50,6 +50,40 @@
     ones = jnp.ones((8, DIM), BF16)
     row = (dot_t(ones, high) + dot_t(ones, low))[0:1]
     return column, row
+
+
+def pack_kernel(*refs):
+    packed_ref, sems = refs[5], refs[11]
+    copies = [pltpu.make_async_copy(refs[n], refs[6 + n], sems.at[n]) for n in range(5)]
+    for copy in copies:
+        copy.start()
+    for n in range(2):
+        copies[n].wait()
+        turned = jnp.swapaxes(refs[6 + n][...].astype(F32), 0, 1)
+        doubled = jnp.broadcast_to(turned[:, None], (PER, 2, PER, DIM)).reshape(SRC, PER, DIM)
+        packed_ref[:, 16 * n : 16 * n + 16, :] = doubled.astype(BF16)
+    copies[2].wait()
+    packed_ref[:, 32:48, :] = jnp.swapaxes(refs[8][...].astype(F32), 0, 1).astype(BF16)
+    copies[3].wait()
+    copies[4].wait()
+    row, col = iota((PER, DIM), 0), iota((PER, DIM), 1)
+    contract = (((0,), (0,)), ((), ()))
+    lanes = lax.dot_general(
+        refs[9][...], (row == col).astype(F32).astype(BF16), contract, preferred_element_type=F32
+    ) + lax.dot_general(
+        refs[10][...], (row + PER == col).astype(F32).astype(BF16), contract, preferred_element_type=F32
+    )
+    packed_ref[:, 48:56, :] = jnp.broadcast_to(lanes[:, None, :], (SRC, 8, DIM)).astype(BF16)
+
+
+def pack(*operands):
+    return pl.pallas_call(
+        pack_kernel,
+        out_shape=jax.ShapeDtypeStruct((SRC, 56, DIM), BF16),
+        in_specs=[pl.BlockSpec(memory_space=pl.ANY)] * 5,
+        out_specs=pl.BlockSpec(memory_space=pltpu.VMEM),
+        scratch_shapes=[pltpu.VMEM(x.shape, x.dtype) for x in operands] + [pltpu.SemaphoreType.DMA((5,))],
+    )(*operands)
 
 
 def dot_pair(a, b):
@@ -172,16 +206,17 @@
 
 
 def after(later, earlier):
-    step = dot3(later[:, :DIM], earlier)
+    step = dot_pair(later[:, :DIM], earlier)
     return jnp.concatenate([step[:, :DIM], step[:, DIM:] + later[:, DIM:]], axis=1)
 
 
 def group_kernel(spot_ref, group_ref, before_ref, upto_ref, total_ref):
     spot = spot_ref[0]
     d_row, d_col = iota((DIM, 2 * DIM), 0), iota((DIM, 2 * DIM), 1)
-    chain = [jnp.where(d_row == d_col, 1.0, 0.0), group_ref[0]]
-    for step in range(1, 4):
-        chain.append(after(group_ref[step], chain[-1]))
+    first = group_ref[0]
+    two = after(group_ref[1], first)
+    late = after(group_ref[3], group_ref[2])
+    chain = [jnp.where(d_row == d_col, 1.0, 0.0), first, two, after(group_ref[2], two), after(late, two)]
     before, upto = chain[0], chain[1]
     for step in range(1, 4):
         before = jnp.where(spot == step, chain[step], before)
@@ -191,11 +226,11 @@
     total_ref[...] = chain[4]
 
 
-def last_kernel(one_ref, two_ref, three_ref, upto_ref, direct_ref, reach_ref, out_ref, state_ref):
-    arriving = dot3(two_ref[:, :DIM], three_ref[...]) + two_ref[:, DIM:]
-    arriving = dot3(one_ref[:, :DIM], arriving) + one_ref[:, DIM:]
-    out_ref[...] = (direct_ref[...] + dot3(reach_ref[...], arriving)).astype(BF16)
-    state_ref[...] = dot3(upto_ref[:, :DIM], arriving) + upto_ref[:, DIM:]
+def last_kernel(near_ref, three_ref, upto_ref, direct_ref, reach_ref, out_ref, state_ref):
+    arriving = dot_pair(near_ref[1, :, :DIM], three_ref[...]) + near_ref[1, :, DIM:]
+    arriving = dot_pair(near_ref[0, :, :DIM], arriving) + near_ref[0, :, DIM:]
+    state_ref[...] = dot_pair(upto_ref[:, :DIM], arriving) + upto_ref[:, DIM:]
+    out_ref[...] = (direct_ref[...] + dot_pair(reach_ref[...], arriving)).astype(BF16)
 
 
 def call(kernel, *shapes):
@@ -221,13 +256,7 @@
 
 
 def per_device(query_heads, key_heads, value_heads, gate_log, beta_rate):
-    grouping = value_heads.shape[1] // query_heads.shape[1]
-    queries = jnp.repeat(jnp.swapaxes(query_heads, 0, 1), grouping, axis=0)
-    keys = jnp.repeat(jnp.swapaxes(key_heads, 0, 1), grouping, axis=0)
-    values = jnp.swapaxes(value_heads, 0, 1)
-    rates = jnp.concatenate([gate_log.T, beta_rate.T], axis=1)[:, None, :]
-    rates = jnp.pad(rates, ((0, 0), (0, 7), (0, DIM - 2 * PER)))
-    packed = jnp.concatenate([queries, keys, values, rates], axis=1)
+    packed = pack(query_heads, key_heads, value_heads, gate_log, beta_rate)
     got = lax.all_to_all(packed, "head", split_axis=0, concat_axis=0, tiled=True)
     pair = ((DIM, 2 * DIM), F32)
     own, solved = call(local_kernel, pair, ((TOK, 2 * DIM), F32))(got)
@@ -236,10 +265,13 @@
     group = lax.all_gather(own, "seq", axis_index_groups=groups)
     spot = (lax.axis_index("seq") % 4).astype(jnp.int32)[None]
     before, upto, total = call(group_kernel, pair, pair, pair)(spot, group)
-    one, two, three = shifted(total, 4), shifted(total, 8), shifted(total[:, DIM:], 12)
+    route = [(i - 4 * (1 + i % 2), i) for i in range(count) if i >= 4 * (1 + i % 2)]
+    mixed = lax.ppermute(total, "seq", route)
+    three = shifted(total[:, DIM:], 12)
     direct, reach = call(readout_kernel, ((TOK, DIM), F32), ((TOK, DIM), F32))(got, solved, before)
+    near = lax.all_gather(mixed, "seq", axis_index_groups=[[i, i + 1] for i in range(0, count, 2)])
     rows, last_state = call(last_kernel, ((TOK, DIM), BF16), ((DIM, DIM), F32))(
-        one, two, three, upto, direct, reach
+        near, three, upto, direct, reach
     )
     head_output = lax.all_to_all(rows, "head", split_axis=0, concat_axis=1, tiled=True)
     return head_output, last_state[None, None]

time: 81.5 us -> 78.5 us (0.963)
  waiting for transfers between devices: 23.2 us -> 20.2 us
  blocking collectives: 25 us -> 27.4 us
  local copies, waits for them, and re-layouts: 2.58 us -> 0.67 us
  Pallas kernels: 7.67 us -> 9.43 us
  starting transfers between devices: 21 us -> 19.7 us
  other arithmetic: 0.91 us -> 0 us
    ppermute x3 -> x1, waiting for transfers between devices: 5.24 us -> 0.01 us  [shifted(): lax.ppermute(block, 'seq', [(i - distance, i) for i in range(distance, co...]
    ppermute x3 -> x1, starting transfers between devices: 5.06 us -> 0.66 us  [shifted(): lax.ppermute(block, 'seq', [(i - distance, i) for i in range(distance, co...]
    ppermute x0 -> x1, starting transfers between devices: none -> 3.11 us  [per_device(): mixed = lax.ppermute(total, 'seq', route)]
    ppermute x0 -> x1, waiting for transfers between devices: none -> 2.16 us  [per_device(): mixed = lax.ppermute(total, 'seq', route)]
    all_gather x0 -> x1, blocking collectives: none -> 2.14 us  [per_device(): lax.all_gather(mixed, 'seq', axis_index_groups=[[i, i + 1] for i in range...]
    pallas_call x0 -> x1, Pallas kernels: none -> 2.04 us  [pack(): pl.pallas_call(pack_kernel, out_shape=jax.ShapeDtypeStruct((SRC, 56, DIM)...]
    unnamed x11 -> x0, local copies, waits for them, and re-layouts: 1.81 us -> none
    concatenate x1 -> x0, other arithmetic: 0.83 us -> none  [per_device(): packed = jnp.concatenate([queries, keys, values, rates], axis=1)]
  transfers between devices with their start and end apart: 4 -> 3, of which waited for: 3 -> 2; matrix products, arithmetic and copies ran while one was open for 0% -> 0% of each run, Pallas kernels for 2% -> 2%
where the time goes in v3:
time: 78.5 us; the launch traced here: 78.1 us
  blocking collectives  27.4 us (35%)
  waiting for transfers between devices  20.2 us (26%)
  starting transfers between devices  19.7 us (25%)
  Pallas kernels  9.43 us (12%)
    all_to_all x1, waiting for transfers between devices, per_device(): lax.all_to_all(packed, 'head', split_axis=0, concat_axis=0, tiled=True)  18 us
    all_to_all x1, blocking collectives, per_device(): lax.all_to_all(rows, 'head', split_axis=0, concat_axis=1, tiled=True)  18 us
    all_to_all x1, starting transfers between devices, per_device(): lax.all_to_all(packed, 'head', split_axis=0, concat_axis=0, tiled=True)  16 us
    pallas_call x4, Pallas kernels, run(): pl.pallas_call(kernel, out_shape=outs, in_specs=[pl.BlockSpec(memory_spac...  7.39 us
    all_gather x1, blocking collectives, per_device(): group = lax.all_gather(own, 'seq', axis_index_groups=groups)  7.32 us
    ppermute x1, starting transfers between devices, per_device(): mixed = lax.ppermute(total, 'seq', route)  3.11 us
    ppermute x1, waiting for transfers between devices, per_device(): mixed = lax.ppermute(total, 'seq', route)  2.16 us
    all_gather x1, blocking collectives, per_device(): lax.all_gather(mixed, 'seq', axis_index_groups=[[i, i + 1] for i in range...  2.14 us
  transfers between devices with their start and end apart: 3, of which 2 were waited for; matrix products, arithmetic and copies ran while one was open for 0% of the time, Pallas kernels for 2%

profile of v3, /device:TPU:4, one launch (start us, length us, event | category | flops | bytes accessed | tf_op | source)
XLA Modules:
  0.0 78.1 jit_solution(5848649578578922952)
XLA Ops:
  0.6 2.0 %shard_map.68 = bf16[32,56,128]{2,1,0:T(8,128)(2,1)} custom-call(bf16[16,16,128]{2,1,0:T(8,128)(2,1)} %refs_0_.1, bf16[16,16,128]{2,1,0:T(8,128)(2,1)} %refs_1_.1, bf16[16,32,128]{2,1,0:T(8,128)(2,1)} %refs_2_.1, bf16[16,32]{1,0:T(8,128)(2,1)} %refs_3_.1, bf16[16,32]{1,0:T(8,128)(2,1)} %refs_4_.1), custom_call_target="tpu_custom_call" | custom-call | tf_op jit(solution)/shard_map/pallas_call | solution.py:80
  2.7 16.0 %all-to-all-start = ((bf16[32,56,128]{2,1,0:T(8,128)(2,1)}), bf16[32,56,128]{2,1,0:T(8,128)(2,1)S(1)}, u32[]{:S(2)}, u32[]{:S(2)}) async-start(bf16[32,56,128]{2,1,0:T(8,128)(2,1)} %shard_map.68), calls=%async_computation | async-start | bytes 917504 | tf_op jit(solution)/shard_map/all_to_all | solution.py:260
  18.7 18.0 %all-to-all-done.got_ref = bf16[32,56,128]{2,1,0:T(8,128)(2,1)S(1)} async-done(((bf16[32,56,128]{2,1,0:T(8,128)(2,1)}), bf16[32,56,128]{2,1,0:T(8,128)(2,1)S(1)}, u32[]{:S(2)}, u32[]{:S(2)}) %all-to-all-start) | async-done | bytes 458784 | tf_op jit(solution)/shard_map/all_to_all | solution.py:260
  36.7 4.2 %shard_map.69 = (f32[128,256]{1,0:T(8,128)S(1)}, f32[512,256]{1,0:T(8,128)S(1)}) custom-call(bf16[32,56,128]{2,1,0:T(8,128)(2,1)S(1)} %all-to-all-done.got_ref), custom_call_target="tpu_custom_call" | custom-call | tf_op jit(solution)/shard_map/pallas_call | solution.py:240
  40.9 7.3 %all-gather = f32[512,256]{1,0:T(8,128)S(1)} all-gather(f32[128,256]{1,0:T(8,128)S(1)} %get-tuple-element.11), channel_id=2, replica_groups={{0,32,64,96},{128,160,192,224},{256,288,320,352},{384,416,448,480},{1,3..., dimensions={0}, use_global_device_ids=true | all-gather | bytes 655360 | tf_op jit(solution)/shard_map/all_gather | solution.py:265
  48.2 0.4 shard_map.70
  48.6 3.1 %collective-permute-start = (f32[128,256]{1,0:T(8,128)S(1)}, f32[128,256]{1,0:T(8,128)S(1)}, u32[]{:S(2)}, u32[]{:S(2)}) collective-permute-start(f32[128,256]{1,0:T(8,128)S(1)} %get-tuple-element.12), channel_id=1, source_target_pairs={{0,128},{64,192},{128,256},{32,288},{192,320},{96,352},{256,384},{... | collective-permute-start | bytes 393224 | tf_op jit(solution)/shard_map/ppermute | solution.py:269
  51.8 0.7 collective-permute-start.1
  52.4 1.6 %shard_map.71 = (f32[512,128]{1,0:T(8,128)S(1)}, f32[512,128]{1,0:T(8,128)S(1)}) custom-call(bf16[32,56,128]{2,1,0:T(8,128)(2,1)S(1)} %all-to-all-done.got_ref, f32[512,256]{1,0:T(8,128)S(1)} %get-tuple-element.14.solved_ref, f32[128,256]{1,0:T(8,128)S(1)} %get-tuple-element.15.before_ref), custom_call_target="tpu_custom_call" | custom-call | tf_op jit(solution)/shard_map/pallas_call | solution.py:240
  54.0 2.2 %collective-permute-done = f32[128,256]{1,0:T(8,128)S(1)} collective-permute-done((f32[128,256]{1,0:T(8,128)S(1)}, f32[128,256]{1,0:T(8,128)S(1)}, u32[]{:S(2)}, u32[]{:S(2)}) %collective-permute-start) | collective-permute-done | bytes 131104 | tf_op jit(solution)/shard_map/ppermute | solution.py:269
  56.2 2.1 %all-gather.1 = f32[256,256]{1,0:T(8,128)S(1)} all-gather(f32[128,256]{1,0:T(8,128)S(1)} %collective-permute-done), channel_id=3, replica_groups={{0,32},{64,96},{128,160},{192,224},{256,288},{320,352},{384,416},{448,4..., dimensions={0}, use_global_device_ids=true | all-gather | bytes 393216 | tf_op jit(solution)/shard_map/all_gather | solution.py:272
  58.3 0.0 collective-permute-done.1.three_ref
  58.3 1.2 %shard_map.72 = (bf16[512,128]{1,0:T(8,128)(2,1)S(1)}, f32[128,128]{1,0:T(8,128)}) custom-call(f32[2,128,256]{2,1,0:T(8,128)S(1)} %bitcast.12, f32[128,128]{1,0:T(8,128)S(1)} %collective-permute-done.1.three_ref, f32[128,256]{1,0:T(8,128)S(1)} %get-tuple-element.13.upto_ref, f32[512,128]{1,0:T(8,128)S(1)} %get-tuple-element.16.direct_ref, ...), custom_call_target="tpu_custom_call" | custom-call | tf_op jit(solution)/shard_map/pallas_call | solution.py:240
  59.5 18.0 %all_to_all.24 = bf16[32,16,128]{2,1,0:T(8,128)(2,1)S(1)} all-to-all(bf16[32,16,128]{2,1,0:T(8,128)(2,1)S(1)} %bitcast.13), channel_id=1, replica_groups=mesh['seq'=16,'head'=32] {'head'}, dimensions={0} | all-to-all | bytes 262144 | tf_op jit(solution)/shard_map/all_to_all | solution.py:276
  77.5 0.7 copy_bitcast_fusion
  (1 shorter events, 0.0 us)
Async XLA Ops:
  2.7 34.0 %all-to-all-start = ((bf16[32,56,128]{2,1,0:T(8,128)(2,1)}), bf16[32,56,128]{2,1,0:T(8,128)(2,1)S(1)}, u32[]{:S(2)}, u32[]{:S(2)}) async-start(bf16[32,56,128]{2,1,0:T(8,128)(2,1)} %shard_map.68), calls=%async_computation | async-start | bytes 917504 | tf_op jit(solution)/shard_map/all_to_all | solution.py:260
  48.6 7.6 %collective-permute-start = (f32[128,256]{1,0:T(8,128)S(1)}, f32[128,256]{1,0:T(8,128)S(1)}, u32[]{:S(2)}, u32[]{:S(2)}) collective-permute-start(f32[128,256]{1,0:T(8,128)S(1)} %get-tuple-element.12), channel_id=1, source_target_pairs={{0,128},{64,192},{128,256},{32,288},{192,320},{96,352},{256,384},{... | collective-permute-start | bytes 393224 | tf_op jit(solution)/shard_map/ppermute | solution.py:269
  51.8 6.6 %collective-permute-start.1 = (f32[128,128]{1,0:T(8,128)S(1)}, f32[128,128]{1,0:T(8,128)S(1)}, u32[]{:S(2)}, u32[]{:S(2)}) collective-permute-start(f32[128,128]{1,0:T(8,128)S(1)} %slice.3), channel_id=1, source_target_pairs={{0,384},{32,416},{64,448},{96,480},{1,385},{33,417},{65,449},{97,4... | collective-permute-start | bytes 196616 | tf_op jit(solution)/shard_map/ppermute | solution.py:255

commit v4 on v3

--- a/solution.py
+++ b/solution.py
@@ -52,6 +52,15 @@
     return column, row
 
 
+def column_sums(x):
+    wide = x.astype(F32)
+    return jnp.sum(wide * wide, axis=1, keepdims=True)
+
+
+def diagonal(square, row, col):
+    return jnp.sum(jnp.where(row == col, square, 0.0), axis=0, keepdims=True)
+
+
 def pack_kernel(*refs):
     packed_ref, sems = refs[5], refs[11]
     copies = [pltpu.make_async_copy(refs[n], refs[6 + n], sems.at[n]) for n in range(5)]
@@ -59,11 +68,10 @@
         copy.start()
     for n in range(2):
         copies[n].wait()
-        turned = jnp.swapaxes(refs[6 + n][...].astype(F32), 0, 1)
-        doubled = jnp.broadcast_to(turned[:, None], (PER, 2, PER, DIM)).reshape(SRC, PER, DIM)
-        packed_ref[:, 16 * n : 16 * n + 16, :] = doubled.astype(BF16)
+        turned = jnp.swapaxes(refs[6 + n][...].astype(F32), 0, 1).astype(BF16).reshape(PER, 8, 2, DIM)
+        packed_ref[:, 8 * n : 8 * n + 8] = jnp.broadcast_to(turned[:, None], (PER, 2, 8, 2, DIM)).reshape(SRC, 8, 2, DIM)
     copies[2].wait()
-    packed_ref[:, 32:48, :] = jnp.swapaxes(refs[8][...].astype(F32), 0, 1).astype(BF16)
+    packed_ref[:, 16:24] = jnp.swapaxes(refs[8][...].astype(F32), 0, 1).astype(BF16).reshape(SRC, 8, 2, DIM)
     copies[3].wait()
     copies[4].wait()
     row, col = iota((PER, DIM), 0), iota((PER, DIM), 1)
@@ -73,13 +81,13 @@
     ) + lax.dot_general(
         refs[10][...], (row + PER == col).astype(F32).astype(BF16), contract, preferred_element_type=F32
     )
-    packed_ref[:, 48:56, :] = jnp.broadcast_to(lanes[:, None, :], (SRC, 8, DIM)).astype(BF16)
+    packed_ref[:, 24] = jnp.broadcast_to(lanes[:, None, :], (SRC, 2, DIM)).astype(BF16)
 
 
 def pack(*operands):
     return pl.pallas_call(
         pack_kernel,
-        out_shape=jax.ShapeDtypeStruct((SRC, 56, DIM), BF16),
+        out_shape=jax.ShapeDtypeStruct((SRC, 25, 2, DIM), BF16),
         in_specs=[pl.BlockSpec(memory_space=pl.ANY)] * 5,
         out_specs=pl.BlockSpec(memory_space=pltpu.VMEM),
         scratch_shapes=[pltpu.VMEM(x.shape, x.dtype) for x in operands] + [pltpu.SemaphoreType.DMA((5,))],
@@ -93,7 +101,7 @@
 
 
 def columns_of(got_ref):
-    lanes = got_ref[:, 48:56, :].astype(F32)[:, 0, :].astype(BF16)
+    lanes = got_ref[:, 24].astype(F32)[:, 0, :].astype(BF16)
     token, source = iota((TOK, SRC), 0), iota((TOK, SRC), 1)
     spread = ((token >> 4) == source).astype(F32).astype(BF16)
     rows = dot1(spread, lanes)
@@ -118,19 +126,29 @@
     return dot1(upto, after1), whole, dot1(upto, after2), row, col
 
 
+def picked(x, width):
+    return jnp.concatenate([x[at : at + width] for at in range(width, DIM, 2 * width)], axis=0)
+
+
+def spread_out(x, width):
+    gap = jnp.zeros((width, x.shape[1]), x.dtype)
+    return jnp.concatenate([y for at in range(0, DIM // 2, width) for y in (gap, x[at : at + width])], axis=0)
+
+
 def local_kernel(got_ref, pair_ref, solved_ref):
     gate, beta = columns_of(got_ref)
-    keys = got_ref[:, 16:32, :].reshape(TOK, DIM)
-    values = got_ref[:, 32:48, :].reshape(TOK, DIM)
+    keys = got_ref[:, 8:16].reshape(TOK, DIM)
+    values = got_ref[:, 16:24].reshape(TOK, DIM)
     d11, d21, d22, row, col = spans(gate)
-    k_col, k_row = row_sums(keys)
-    inv_col, inv_row = inv_norm(k_col), inv_norm(k_row)
+    inv_col = inv_norm(column_sums(keys))
     strict = row > col
     scale = beta * inv_col
     k1, k2 = keys[:HALF], keys[HALF:]
-    l11 = jnp.where(strict, scale[:HALF] * jnp.exp(jnp.where(strict, d11, 0.0)) * dot_t(k1, k1) * inv_row[:, :HALF], 0.0)
-    l22 = jnp.where(strict, scale[HALF:] * jnp.exp(jnp.where(strict, d22, 0.0)) * dot_t(k2, k2) * inv_row[:, HALF:], 0.0)
-    l21 = scale[HALF:] * jnp.exp(d21) * dot_t(k2, k1) * inv_row[:, :HALF]
+    kk1, kk2 = dot_t(k1, k1), dot_t(k2, k2)
+    inv1, inv2 = inv_norm(diagonal(kk1, row, col)), inv_norm(diagonal(kk2, row, col))
+    l11 = jnp.where(strict, scale[:HALF] * jnp.exp(jnp.where(strict, d11, 0.0)) * kk1 * inv1, 0.0)
+    l22 = jnp.where(strict, scale[HALF:] * jnp.exp(jnp.where(strict, d22, 0.0)) * kk2 * inv2, 0.0)
+    l21 = scale[HALF:] * jnp.exp(d21) * dot_t(k2, k1) * inv1
     cumul = jnp.concatenate([d11[:, :1], d21[:, :1]], axis=0) + gate[:1]
     gate_wide = jnp.broadcast_to(gate, (TOK, DIM)).astype(BF16)
     later = (row < col).astype(F32).astype(BF16)
@@ -155,9 +173,11 @@
     n8 = [dot_pair(n, n) for n in n4]
     x = [y + dot_pair(y, n) for y, n in zip(x, n8)]
     for width in (16, 32, 64):
-        here = (apart >= width) & (apart < 2 * width)
-        half = [dot_pair(jnp.where(here, b, 0.0), y) for b, y in zip(blocks, x)]
-        x = [y - dot_pair(y, z) for y, z in zip(x, half)]
+        here = picked(apart, width)
+        here = (here >= width) & (here < 2 * width)
+        half = [dot_pair(jnp.where(here, picked(b, width), 0.0), y) for b, y in zip(blocks, x)]
+        step = [dot_pair(picked(y, width), spread_out(z, width)) for y, z in zip(x, half)]
+        x = [y - spread_out(z, width) for y, z in zip(x, step)]
     merged = []
     for lo, hi, tie in ((x[0], x[1], l11[DIM:, :DIM]), (x[2], x[3], l22[DIM:, :DIM])):
         cross = -dot_pair(hi, dot_pair(tie, lo))
@@ -182,8 +202,8 @@
 
 def readout_kernel(got_ref, solved_ref, before_ref, direct_ref, reach_ref):
     gate, _ = columns_of(got_ref)
-    queries = got_ref[:, 0:16, :].reshape(TOK, DIM)
-    keys = got_ref[:, 16:32, :].reshape(TOK, DIM)
+    queries = got_ref[:, 0:8].reshape(TOK, DIM)
+    keys = got_ref[:, 8:16].reshape(TOK, DIM)
     d11, d21, d22, row, col = spans(gate)
     q_col, _ = row_sums(queries)
     _, k_row = row_sums(keys)

time: 78.5 us -> 77.4 us (0.986)
  waiting for transfers between devices: 20.2 us -> 19 us
    all_to_all x1, waiting for transfers between devices: 18 us -> 17.2 us  [per_device(): lax.all_to_all(packed, 'head', split_axis=0, concat_axis=0, tiled=True)]
  transfers between devices with their start and end apart: 3 -> 3, of which waited for: 2 -> 2; matrix products, arithmetic and copies ran while one was open for 0% -> 0% of each run, Pallas kernels for 2% -> 3%
where the time goes in v4:
time: 77.4 us; the launch traced here: 77.1 us
  blocking collectives  27.1 us (35%)
  starting transfers between devices  19.7 us (25%)
  waiting for transfers between devices  19 us (25%)
  Pallas kernels  9.83 us (13%)
    all_to_all x1, blocking collectives, per_device(): lax.all_to_all(rows, 'head', split_axis=0, concat_axis=1, tiled=True)  17.8 us
    all_to_all x1, waiting for transfers between devices, per_device(): lax.all_to_all(packed, 'head', split_axis=0, concat_axis=0, tiled=True)  17.2 us
    all_to_all x1, starting transfers between devices, per_device(): lax.all_to_all(packed, 'head', split_axis=0, concat_axis=0, tiled=True)  16 us
    pallas_call x4, Pallas kernels, run(): pl.pallas_call(kernel, out_shape=outs, in_specs=[pl.BlockSpec(memory_spac...  7.71 us
    all_gather x1, blocking collectives, per_device(): group = lax.all_gather(own, 'seq', axis_index_groups=groups)  7.15 us
    ppermute x1, starting transfers between devices, per_device(): mixed = lax.ppermute(total, 'seq', route)  3.11 us
    all_gather x1, blocking collectives, per_device(): lax.all_gather(mixed, 'seq', axis_index_groups=[[i, i + 1] for i in range...  2.14 us
    pallas_call x1, Pallas kernels, pack(): pl.pallas_call(pack_kernel, out_shape=jax.ShapeDtypeStruct((SRC, 25, 2, D...  2.12 us
  transfers between devices with their start and end apart: 3, of which 2 were waited for; matrix products, arithmetic and copies ran while one was open for 0% of the time, Pallas kernels for 3%

profile of v4, /device:TPU:4, one launch (start us, length us, event | category | flops | bytes accessed | tf_op | source)
XLA Modules:
  0.0 77.1 jit_solution(95868058159125732)
XLA Ops:
  0.6 2.1 %shard_map.68 = bf16[32,25,2,128]{3,2,1,0:T(2,128)(2,1)} custom-call(bf16[16,16,128]{2,1,0:T(8,128)(2,1)} %refs_0_.1, bf16[16,16,128]{2,1,0:T(8,128)(2,1)} %refs_1_.1, bf16[16,32,128]{2,1,0:T(8,128)(2,1)} %refs_2_.1, bf16[16,32]{1,0:T(8,128)(2,1)} %refs_3_.1, bf16[16,32]{1,0:T(8,128)(2,1)} %refs_4_.1), custom_call_target="tpu_custom_call" | custom-call | tf_op jit(solution)/shard_map/pallas_call | solution.py:88
  2.8 16.0 %all-to-all-start = ((bf16[32,25,2,128]{3,2,1,0:T(2,128)(2,1)}), bf16[32,25,2,128]{3,2,1,0:T(2,128)(2,1)S(1)}, u32[]{:S(2)}, u32[]{:S(2)}) async-start(bf16[32,25,2,128]{3,2,1,0:T(2,128)(2,1)} %shard_map.68), calls=%async_computation | async-start | bytes 819200 | tf_op jit(solution)/shard_map/all_to_all | solution.py:280
  18.7 17.2 %all-to-all-done.got_ref = bf16[32,25,2,128]{3,2,1,0:T(2,128)(2,1)S(1)} async-done(((bf16[32,25,2,128]{3,2,1,0:T(2,128)(2,1)}), bf16[32,25,2,128]{3,2,1,0:T(2,128)(2,1)S(1)}, u32[]{:S(2)}, u32[]{:S(2)}) %all-to-all-start) | async-done | bytes 409632 | tf_op jit(solution)/shard_map/all_to_all | solution.py:280
  35.9 4.1 %shard_map.69 = (f32[128,256]{1,0:T(8,128)S(1)}, f32[512,256]{1,0:T(8,128)S(1)}) custom-call(bf16[32,25,2,128]{3,2,1,0:T(2,128)(2,1)S(1)} %all-to-all-done.got_ref), custom_call_target="tpu_custom_call" | custom-call | tf_op jit(solution)/shard_map/pallas_call | solution.py:260
  40.1 7.1 %all-gather = f32[512,256]{1,0:T(8,128)S(1)} all-gather(f32[128,256]{1,0:T(8,128)S(1)} %get-tuple-element.11), channel_id=2, replica_groups={{0,32,64,96},{128,160,192,224},{256,288,320,352},{384,416,448,480},{1,3..., dimensions={0}, use_global_device_ids=true | all-gather | bytes 655360 | tf_op jit(solution)/shard_map/all_gather | solution.py:285
  47.2 0.4 shard_map.70
  47.7 3.1 %collective-permute-start = (f32[128,256]{1,0:T(8,128)S(1)}, f32[128,256]{1,0:T(8,128)S(1)}, u32[]{:S(2)}, u32[]{:S(2)}) collective-permute-start(f32[128,256]{1,0:T(8,128)S(1)} %get-tuple-element.12), channel_id=1, source_target_pairs={{0,128},{64,192},{128,256},{32,288},{192,320},{96,352},{256,384},{... | collective-permute-start | bytes 393224 | tf_op jit(solution)/shard_map/ppermute | solution.py:289
  50.8 0.7 collective-permute-start.1
  51.5 2.0 %shard_map.71 = (f32[512,128]{1,0:T(8,128)S(1)}, f32[512,128]{1,0:T(8,128)S(1)}) custom-call(bf16[32,25,2,128]{3,2,1,0:T(2,128)(2,1)S(1)} %all-to-all-done.got_ref, f32[512,256]{1,0:T(8,128)S(1)} %get-tuple-element.14.solved_ref, f32[128,256]{1,0:T(8,128)S(1)} %get-tuple-element.15.before_ref), custom_call_target="tpu_custom_call" | custom-call | tf_op jit(solution)/shard_map/pallas_call | solution.py:260
  53.4 1.8 %collective-permute-done = f32[128,256]{1,0:T(8,128)S(1)} collective-permute-done((f32[128,256]{1,0:T(8,128)S(1)}, f32[128,256]{1,0:T(8,128)S(1)}, u32[]{:S(2)}, u32[]{:S(2)}) %collective-permute-start) | collective-permute-done | bytes 131104 | tf_op jit(solution)/shard_map/ppermute | solution.py:289
  55.2 2.1 %all-gather.1 = f32[256,256]{1,0:T(8,128)S(1)} all-gather(f32[128,256]{1,0:T(8,128)S(1)} %collective-permute-done), channel_id=3, replica_groups={{0,32},{64,96},{128,160},{192,224},{256,288},{320,352},{384,416},{448,4..., dimensions={0}, use_global_device_ids=true | all-gather | bytes 393216 | tf_op jit(solution)/shard_map/all_gather | solution.py:292
  57.4 0.0 collective-permute-done.1.three_ref
  57.4 1.2 %shard_map.72 = (bf16[512,128]{1,0:T(8,128)(2,1)S(1)}, f32[128,128]{1,0:T(8,128)}) custom-call(f32[2,128,256]{2,1,0:T(8,128)S(1)} %bitcast.12, f32[128,128]{1,0:T(8,128)S(1)} %collective-permute-done.1.three_ref, f32[128,256]{1,0:T(8,128)S(1)} %get-tuple-element.13.upto_ref, f32[512,128]{1,0:T(8,128)S(1)} %get-tuple-element.16.direct_ref, ...), custom_call_target="tpu_custom_call" | custom-call | tf_op jit(solution)/shard_map/pallas_call | solution.py:260
  58.6 17.8 %all_to_all.24 = bf16[32,16,128]{2,1,0:T(8,128)(2,1)S(1)} all-to-all(bf16[32,16,128]{2,1,0:T(8,128)(2,1)S(1)} %bitcast.13), channel_id=1, replica_groups=mesh['seq'=16,'head'=32] {'head'}, dimensions={0} | all-to-all | bytes 262144 | tf_op jit(solution)/shard_map/all_to_all | solution.py:296
  76.4 0.7 copy_bitcast_fusion
  (1 shorter events, 0.0 us)
Async XLA Ops:
  2.8 33.2 %all-to-all-start = ((bf16[32,25,2,128]{3,2,1,0:T(2,128)(2,1)}), bf16[32,25,2,128]{3,2,1,0:T(2,128)(2,1)S(1)}, u32[]{:S(2)}, u32[]{:S(2)}) async-start(bf16[32,25,2,128]{3,2,1,0:T(2,128)(2,1)} %shard_map.68), calls=%async_computation | async-start | bytes 819200 | tf_op jit(solution)/shard_map/all_to_all | solution.py:280
  47.7 7.6 %collective-permute-start = (f32[128,256]{1,0:T(8,128)S(1)}, f32[128,256]{1,0:T(8,128)S(1)}, u32[]{:S(2)}, u32[]{:S(2)}) collective-permute-start(f32[128,256]{1,0:T(8,128)S(1)} %get-tuple-element.12), channel_id=1, source_target_pairs={{0,128},{64,192},{128,256},{32,288},{192,320},{96,352},{256,384},{... | collective-permute-start | bytes 393224 | tf_op jit(solution)/shard_map/ppermute | solution.py:289
  50.8 6.6 %collective-permute-start.1 = (f32[128,128]{1,0:T(8,128)S(1)}, f32[128,128]{1,0:T(8,128)S(1)}, u32[]{:S(2)}, u32[]{:S(2)}) collective-permute-start(f32[128,128]{1,0:T(8,128)S(1)} %slice.3), channel_id=1, source_target_pairs={{0,384},{32,416},{64,448},{96,480},{1,385},{33,417},{65,449},{97,4... | collective-permute-start | bytes 196616 | tf_op jit(solution)/shard_map/ppermute | solution.py:275

commit v5 on v4

v5 whole, which is shorter than its diff:
```python
import jax
import jax.numpy as jnp
from jax import lax
from jax.experimental import pallas as pl
from jax.experimental.pallas import tpu as pltpu
from jax.sharding import PartitionSpec as P

F32 = jnp.float32
BF16 = jnp.bfloat16
TOK = 512
DIM = 128
SRC = 32
PER = 16
HALF = 256


def iota(shape, dim):
    return lax.broadcasted_iota(jnp.int32, shape, dim)


def dot1(a, b):
    return lax.dot_general(a, b, (((1,), (0,)), ((), ())), preferred_element_type=F32)


def dot_t(a, b):
    return lax.dot_general(a, b, (((1,), (1,)), ((), ())), preferred_element_type=F32)


def split(a):
    high = a.astype(BF16)
    return high, (a - high.astype(F32)).astype(BF16)


def dot3(a, b):
    ah, al = split(a)
    bh, bl = split(b)
    return dot1(ah, bh) + (dot1(ah, bl) + dot1(al, bh))


def inv_norm(total):
    total = total + 1e-6
    y = lax.rsqrt(total)
    return y * (1.5 - 0.5 * total * y * y)


def row_sums(x):
    squares = x.astype(F32) * x.astype(F32)
    column = jnp.sum(squares, axis=1, keepdims=True)
    high, low = split(squares)
    ones = jnp.ones((8, DIM), BF16)
    row = (dot_t(ones, high) + dot_t(ones, low))[0:1]
    return column, row


def column_sums(x):
    wide = x.astype(F32)
    return jnp.sum(wide * wide, axis=1, keepdims=True)


def diagonal(square, row, col):
    return jnp.sum(jnp.where(row == col, square, 0.0), axis=0, keepdims=True)


def pack_kernel(*refs):
    packed_ref, ins, parts, sems, gone = refs[5], refs[6:11], refs[11:15], refs[15], refs[16]
    copies = [pltpu.make_async_copy(refs[n], ins[n], sems.at[n]) for n in range(5)]
    sent = [
        pltpu.make_async_copy(part, packed_ref.at[:, 8 * n : 8 * n + part.shape[1]], gone.at[n])
        for n, part in enumerate(parts)
    ]
    for n in (3, 4, 2, 0, 1):
        copies[n].start()
    copies[3].wait()
    copies[4].wait()
    row, col = iota((PER, DIM), 0), iota((PER, DIM), 1)
    contract = (((0,), (0,)), ((), ()))
    lanes = lax.dot_general(
        ins[3][...], (row == col).astype(F32).astype(BF16), contract, preferred_element_type=F32
    ) + lax.dot_general(
        ins[4][...], (row + PER == col).astype(F32).astype(BF16), contract, preferred_element_type=F32
    )
    parts[3][:, 0] = jnp.broadcast_to(lanes[:, None, :], (SRC, 2, DIM)).astype(BF16)
    sent[3].start()
    copies[2].wait()
    parts[2][...] = jnp.swapaxes(ins[2][...].astype(F32), 0, 1).astype(BF16).reshape(SRC, 8, 2, DIM)
    sent[2].start()
    for n in range(2):
        copies[n].wait()
        turned = jnp.swapaxes(ins[n][...].astype(F32), 0, 1).astype(BF16).reshape(PER, 8, 2, DIM)
        parts[n][...] = jnp.broadcast_to(turned[:, None], (PER, 2, 8, 2, DIM)).reshape(SRC, 8, 2, DIM)
        sent[n].start()
    for copy in sent:
        copy.wait()


def pack(*operands):
    hbm = pl.BlockSpec(memory_space=pl.ANY)
    return pl.pallas_call(
        pack_kernel,
        out_shape=jax.ShapeDtypeStruct((SRC, 25, 2, DIM), BF16),
        in_specs=[hbm] * 5,
        out_specs=hbm,
        scratch_shapes=[pltpu.VMEM(x.shape, x.dtype) for x in operands]
        + [pltpu.VMEM((SRC, n, 2, DIM), BF16) for n in (8, 8, 8, 1)]
        + [pltpu.SemaphoreType.DMA((5,)), pltpu.SemaphoreType.DMA((4,))],
    )(*operands)


def dot_pair(a, b):
    ah, al = split(a)
    bh, bl = split(b)
    return dot1(jnp.concatenate([ah, al], axis=1), jnp.concatenate([bh, bh], axis=0)) + dot1(ah, bl)


def columns_of(got_ref):
    lanes = got_ref[:, 24].astype(F32)[:, 0, :].astype(BF16)
    token, source = iota((TOK, SRC), 0), iota((TOK, SRC), 1)
    spread = ((token >> 4) == source).astype(F32).astype(BF16)
    rows = dot1(spread, lanes)
    lane = iota((TOK, DIM), 1)
    spot = iota((TOK, DIM), 0) & (PER - 1)
    gate = jnp.sum(jnp.where(lane == spot, rows, 0.0), axis=1, keepdims=True)
    beta = jnp.sum(jnp.where(lane == spot + PER, rows, 0.0), axis=1, keepdims=True)
    return gate, beta


def chunks(x):
    return [x[at : at + DIM] for at in range(0, TOK, DIM)]


def spans(gate):
    row, col = iota((DIM, DIM), 0), iota((DIM, DIM), 1)
    upto = (row >= col).astype(F32).astype(BF16)
    steps = chunks(gate)
    after_all = jnp.concatenate([jnp.where(row > col, g, 0.0).astype(BF16) for g in steps], axis=1)
    wide = dot1(upto, after_all)
    differ = [wide[:, at : at + DIM] for at in range(0, TOK, DIM)]
    return differ, [d[:, :1] + g[:1] for d, g in zip(differ, steps)], row, col


def picked(x, width):
    return jnp.concatenate([x[at : at + width] for at in range(width, DIM, 2 * width)], axis=0)


def spread_out(x, width):
    gap = jnp.zeros((width, x.shape[1]), x.dtype)
    return jnp.concatenate([y for at in range(0, DIM // 2, width) for y in (gap, x[at : at + width])], axis=0)


def after(later, earlier):
    step = dot_pair(later[:, :DIM], earlier)
    return jnp.concatenate([step[:, :DIM], step[:, DIM:] + later[:, DIM:]], axis=1)


def local_kernel(got_ref, pair_ref, solved_ref, maps_ref):
    gate, beta = columns_of(got_ref)
    keys = got_ref[:, 8:16].reshape(TOK, DIM)
    values = got_ref[:, 16:24].reshape(TOK, DIM)
    differ, cumul, row, col = spans(gate)
    key_inv = inv_norm(column_sums(keys))
    strict = row > col
    later = (row < col).astype(F32).astype(BF16)
    gates = jnp.concatenate([jnp.broadcast_to(g, (DIM, DIM)).astype(BF16) for g in chunks(gate)], axis=1)
    beyond = dot1(later, gates)
    keys, values, scale, beta, key_inv = (chunks(x) for x in (keys, values, beta * key_inv, beta, key_inv))
    blocks, right = [], []
    for k, v, d, c, sc, b in zip(keys, values, differ, cumul, scale, beta):
        key_key = dot_t(k, k)
        inv_row = inv_norm(diagonal(key_key, row, col))
        blocks.append(jnp.where(strict, sc * jnp.exp(jnp.where(strict, d, 0.0)) * key_key * inv_row, 0.0))
        right.append(jnp.concatenate([(sc * jnp.exp(c)) * k.astype(F32), b * v.astype(F32)], axis=1))
    apart = row ^ col
    eye = jnp.where(apart == 0, 1.0, 0.0)
    n1 = [jnp.where(apart < 16, -b, 0.0) for b in blocks]
    n2 = [dot_pair(n, n) for n in n1]
    x = [eye + n + m + dot_pair(n, m) for n, m in zip(n1, n2)]
    n4 = [dot_pair(n, n) for n in n2]
    x = [y + dot_pair(y, n) for y, n in zip(x, n4)]
    n8 = [dot_pair(n, n) for n in n4]
    x = [y + dot_pair(y, n) for y, n in zip(x, n8)]
    for width in (16, 32, 64):
        here = picked(apart, width)
        here = (here >= width) & (here < 2 * width)
        half = [dot_pair(jnp.where(here, picked(b, width), 0.0), y) for b, y in zip(blocks, x)]
        step = [dot_pair(picked(y, width), spread_out(z, width)) for y, z in zip(x, half)]
        x = [y - spread_out(z, width) for y, z in zip(x, step)]
    maps = []
    for at in range(4):
        solved = dot_pair(x[at], right[at])
        solved_ref[DIM * at : DIM * at + DIM, :] = solved
        weight = key_inv[at] * jnp.exp(beyond[:, DIM * at : DIM * at + DIM])
        high, low = split(jnp.concatenate([weight, weight], axis=1) * solved)
        keys_t = keys[at].T
        moved = dot1(jnp.concatenate([keys_t, keys_t], axis=1), jnp.concatenate([high, low], axis=0))
        kept = jnp.where(apart == 0, jnp.exp(cumul[at][DIM - 1 :]), 0.0)
        maps.append(jnp.concatenate([kept - moved[:, :DIM], moved[:, DIM:]], axis=1))
    early, late = after(maps[1], maps[0]), after(maps[3], maps[2])
    pair_ref[...] = after(late, early)
    maps_ref[0] = maps[0]
    maps_ref[1] = early
    maps_ref[2] = maps[2]


def readout_kernel(got_ref, solved_ref, maps_ref, before_ref, direct_ref, reach_ref):
    gate, _ = columns_of(got_ref)
    queries = got_ref[:, 0:8].reshape(TOK, DIM)
    keys = got_ref[:, 8:16].reshape(TOK, DIM)
    differ, cumul, row, col = spans(gate)
    query_inv = chunks(inv_norm(column_sums(queries)))
    inclusive = row >= col
    first = before_ref[...]
    half = after(maps_ref[1], first)
    starts = [first, after(maps_ref[0], first), half, after(maps_ref[2], half)]
    for at, (q, k, d, c, i, start) in enumerate(zip(chunks(queries), chunks(keys), differ, cumul, query_inv, starts)):
        key_inv = inv_norm(diagonal(dot_t(k, k), row, col))
        scores = jnp.where(inclusive, i * jnp.exp(jnp.where(inclusive, d, 0.0)) * dot_t(q, k) * key_inv, 0.0)
        span = slice(DIM * at, DIM * at + DIM)
        mixed = dot_pair(scores, solved_ref[span, :])
        step = dot_pair(i * jnp.exp(c) * q.astype(F32) - mixed[:, :DIM], start)
        reach_ref[span, :] = step[:, :DIM]
        direct_ref[span, :] = mixed[:, DIM:] + step[:, DIM:]


def group_kernel(spot_ref, group_ref, before_ref, upto_ref, total_ref):
    spot = spot_ref[0]
    d_row, d_col = iota((DIM, 2 * DIM), 0), iota((DIM, 2 * DIM), 1)
    first = group_ref[0]
    two = after(group_ref[1], first)
    late = after(group_ref[3], group_ref[2])
    chain = [jnp.where(d_row == d_col, 1.0, 0.0), first, two, after(group_ref[2], two), after(late, two)]
    before, upto = chain[0], chain[1]
    for step in range(1, 4):
        before = jnp.where(spot == step, chain[step], before)
        upto = jnp.where(spot == step, chain[step + 1], upto)
    before_ref[...] = before
    upto_ref[...] = upto
    total_ref[...] = chain[4]


def last_kernel(near_ref, three_ref, upto_ref, direct_ref, reach_ref, out_ref, state_ref):
    arriving = dot_pair(near_ref[1, :, :DIM], three_ref[...]) + near_ref[1, :, DIM:]
    arriving = dot_pair(near_ref[0, :, :DIM], arriving) + near_ref[0, :, DIM:]
    state_ref[...] = dot_pair(upto_ref[:, :DIM], arriving) + upto_ref[:, DIM:]
    out_ref[...] = (direct_ref[...] + dot_pair(reach_ref[...], arriving)).astype(BF16)


def call(kernel, *shapes):
    def run(*operands):
        vmem = pl.BlockSpec(memory_space=pltpu.VMEM)
        outs = tuple(jax.ShapeDtypeStruct(shape, dtype) for shape, dtype in shapes)
        return pl.pallas_call(
            kernel,
            out_shape=outs,
            in_specs=[
                pl.BlockSpec(memory_space=pltpu.SMEM) if x.dtype == jnp.int32 else vmem for x in operands
            ],
            out_specs=tuple([vmem] * len(outs)),
            compiler_params=pltpu.CompilerParams(vmem_limit_bytes=48 << 20),
        )(*operands)

    return run


def shifted(block, distance):
    count = lax.axis_size("seq")
    return lax.ppermute(block, "seq", [(i - distance, i) for i in range(distance, count)])


def per_device(query_heads, key_heads, value_heads, gate_log, beta_rate):
    packed = pack(query_heads, key_heads, value_heads, gate_log, beta_rate)
    got = lax.all_to_all(packed, "head", split_axis=0, concat_axis=0, tiled=True)
    pair = ((DIM, 2 * DIM), F32)
    own, solved, maps = call(local_kernel, pair, ((TOK, 2 * DIM), F32), ((3, DIM, 2 * DIM), F32))(got)
    count = lax.axis_size("seq")
    groups = [list(range(first, first + 4)) for first in range(0, count, 4)]
    group = lax.all_gather(own, "seq", axis_index_groups=groups)
    spot = (lax.axis_index("seq") % 4).astype(jnp.int32)[None]
    before, upto, total = call(group_kernel, pair, pair, pair)(spot, group)
    route = [(i - 4 * (1 + i % 2), i) for i in range(count) if i >= 4 * (1 + i % 2)]
    mixed = lax.ppermute(total, "seq", route)
    three = shifted(total[:, DIM:], 12)
    direct, reach = call(readout_kernel, ((TOK, DIM), F32), ((TOK, DIM), F32))(got, solved, maps, before)
    near = lax.all_gather(mixed, "seq", axis_index_groups=[[i, i + 1] for i in range(0, count, 2)])
    rows, last_state = call(last_kernel, ((TOK, DIM), BF16), ((DIM, DIM), F32))(
        near, three, upto, direct, reach
    )
    head_output = lax.all_to_all(rows, "head", split_axis=0, concat_axis=1, tiled=True)
    return head_output, last_state[None, None]


def solution(mesh):
    return jax.shard_map(
        per_device,
        mesh=mesh,
        in_specs=(
            P(("seq", "head"), None, None),
            P(("seq", "head"), None, None),
            P(("seq", "head"), None, None),
            P(("seq", "head"), None),
            P(("seq", "head"), None),
        ),
        out_specs=(P(("seq", "head"), None), P("seq", "head", None, None)),
        check_vma=False,
    )
```

time: 77.4 us -> 77.1 us (level)
  no operation moved by 1% of the time
where the time goes in v5:
time: 77.1 us; the launch traced here: 76.7 us
  blocking collectives  27 us (35%)
  starting transfers between devices  19.7 us (26%)
  waiting for transfers between devices  19 us (25%)
  Pallas kernels  9.53 us (12%)
    all_to_all x1, blocking collectives, per_device(): lax.all_to_all(rows, 'head', split_axis=0, concat_axis=1, tiled=True)  17.8 us
    all_to_all x1, waiting for transfers between devices, per_device(): lax.all_to_all(packed, 'head', split_axis=0, concat_axis=0, tiled=True)  17.2 us
    all_to_all x1, starting transfers between devices, per_device(): lax.all_to_all(packed, 'head', split_axis=0, concat_axis=0, tiled=True)  16 us
    pallas_call x4, Pallas kernels, run(): pl.pallas_call(kernel, out_shape=outs, in_specs=[pl.BlockSpec(memory_spac...  7.53 us
    all_gather x1, blocking collectives, per_device(): group = lax.all_gather(own, 'seq', axis_index_groups=groups)  7.15 us
    ppermute x1, starting transfers between devices, per_device(): mixed = lax.ppermute(total, 'seq', route)  3.1 us
    all_gather x1, blocking collectives, per_device(): lax.all_gather(mixed, 'seq', axis_index_groups=[[i, i + 1] for i in range...  2.05 us
    pallas_call x1, Pallas kernels, pack(): pl.pallas_call(pack_kernel, out_shape=jax.ShapeDtypeStruct((SRC, 25, 2, D...  2 us
  transfers between devices with their start and end apart: 3, of which 2 were waited for; matrix products, arithmetic and copies ran while one was open for 0% of the time, Pallas kernels for 3%

profile of v5, /device:TPU:4, one launch (start us, length us, event | category | flops | bytes accessed | tf_op | source)
XLA Modules:
  0.0 76.7 jit_solution(11722347085946685836)
XLA Ops:
  0.6 2.0 %shard_map.68 = bf16[32,25,2,128]{3,2,1,0:T(2,128)(2,1)} custom-call(bf16[16,16,128]{2,1,0:T(8,128)(2,1)} %refs_0_.1, bf16[16,16,128]{2,1,0:T(8,128)(2,1)} %refs_1_.1, bf16[16,32,128]{2,1,0:T(8,128)(2,1)} %refs_2_.1, bf16[16,32]{1,0:T(8,128)(2,1)} %refs_3_.1, bf16[16,32]{1,0:T(8,128)(2,1)} %refs_4_.1), custom_call_target="tpu_custom_call" | custom-call | tf_op jit(solution)/shard_map/pallas_call | solution.py:98
  2.6 16.0 %all-to-all-start = ((bf16[32,25,2,128]{3,2,1,0:T(2,128)(2,1)}), bf16[32,25,2,128]{3,2,1,0:T(2,128)(2,1)S(1)}, u32[]{:S(2)}, u32[]{:S(2)}) async-start(bf16[32,25,2,128]{3,2,1,0:T(2,128)(2,1)} %shard_map.68), calls=%async_computation | async-start | bytes 819200 | tf_op jit(solution)/shard_map/all_to_all | solution.py:271
  18.6 17.2 %all-to-all-done.got_ref = bf16[32,25,2,128]{3,2,1,0:T(2,128)(2,1)S(1)} async-done(((bf16[32,25,2,128]{3,2,1,0:T(2,128)(2,1)}), bf16[32,25,2,128]{3,2,1,0:T(2,128)(2,1)S(1)}, u32[]{:S(2)}, u32[]{:S(2)}) %all-to-all-start) | async-done | bytes 409632 | tf_op jit(solution)/shard_map/all_to_all | solution.py:271
  35.8 3.9 %shard_map.69 = (f32[128,256]{1,0:T(8,128)S(1)}, f32[512,256]{1,0:T(8,128)S(1)}, f32[3,128,256]{2,1,0:T(8,128)S(1)}) custom-call(bf16[32,25,2,128]{3,2,1,0:T(2,128)(2,1)S(1)} %all-to-all-done.got_ref), custom_call_target="tpu_custom_call" | custom-call | tf_op jit(solution)/shard_map/pallas_call | solution.py:251
  39.8 7.1 %all-gather = f32[512,256]{1,0:T(8,128)S(1)} all-gather(f32[128,256]{1,0:T(8,128)S(1)} %get-tuple-element.12), channel_id=2, replica_groups={{0,32,64,96},{128,160,192,224},{256,288,320,352},{384,416,448,480},{1,3..., dimensions={0}, use_global_device_ids=true | all-gather | bytes 655360 | tf_op jit(solution)/shard_map/all_gather | solution.py:276
  46.9 0.4 shard_map.70
  47.3 3.1 %collective-permute-start = (f32[128,256]{1,0:T(8,128)S(1)}, f32[128,256]{1,0:T(8,128)S(1)}, u32[]{:S(2)}, u32[]{:S(2)}) collective-permute-start(f32[128,256]{1,0:T(8,128)S(1)} %get-tuple-element.13), channel_id=1, source_target_pairs={{0,128},{64,192},{128,256},{32,288},{192,320},{96,352},{256,384},{... | collective-permute-start | bytes 393224 | tf_op jit(solution)/shard_map/ppermute | solution.py:280
  50.5 0.7 collective-permute-start.1
  51.1 2.0 %shard_map.71 = (f32[512,128]{1,0:T(8,128)S(1)}, f32[512,128]{1,0:T(8,128)S(1)}) custom-call(bf16[32,25,2,128]{3,2,1,0:T(2,128)(2,1)S(1)} %all-to-all-done.got_ref, f32[512,256]{1,0:T(8,128)S(1)} %get-tuple-element.15.solved_ref, f32[3,128,256]{2,1,0:T(8,128)S(1)} %get-tuple-element.16.maps_ref, f32[128,256]{1,0:T(8,128)S(1)} %get-tuple-element.17.before_ref), custom_call_target="tpu_custom_call" | custom-call | tf_op jit(solution)/shard_map/pallas_call | solution.py:251
  53.1 1.9 %collective-permute-done = f32[128,256]{1,0:T(8,128)S(1)} collective-permute-done((f32[128,256]{1,0:T(8,128)S(1)}, f32[128,256]{1,0:T(8,128)S(1)}, u32[]{:S(2)}, u32[]{:S(2)}) %collective-permute-start) | collective-permute-done | bytes 131104 | tf_op jit(solution)/shard_map/ppermute | solution.py:280
  55.0 2.0 %all-gather.1 = f32[256,256]{1,0:T(8,128)S(1)} all-gather(f32[128,256]{1,0:T(8,128)S(1)} %collective-permute-done), channel_id=3, replica_groups={{0,32},{64,96},{128,160},{192,224},{256,288},{320,352},{384,416},{448,4..., dimensions={0}, use_global_device_ids=true | all-gather | bytes 393216 | tf_op jit(solution)/shard_map/all_gather | solution.py:283
  57.0 0.0 collective-permute-done.1.three_ref
  57.0 1.2 %shard_map.72 = (bf16[512,128]{1,0:T(8,128)(2,1)S(1)}, f32[128,128]{1,0:T(8,128)}) custom-call(f32[2,128,256]{2,1,0:T(8,128)S(1)} %bitcast.12, f32[128,128]{1,0:T(8,128)S(1)} %collective-permute-done.1.three_ref, f32[128,256]{1,0:T(8,128)S(1)} %get-tuple-element.14.upto_ref, f32[512,128]{1,0:T(8,128)S(1)} %get-tuple-element.18.direct_ref, ...), custom_call_target="tpu_custom_call" | custom-call | tf_op jit(solution)/shard_map/pallas_call | solution.py:251
  58.2 17.8 %all_to_all.24 = bf16[32,16,128]{2,1,0:T(8,128)(2,1)S(1)} all-to-all(bf16[32,16,128]{2,1,0:T(8,128)(2,1)S(1)} %bitcast.13), channel_id=1, replica_groups=mesh['seq'=16,'head'=32] {'head'}, dimensions={0} | all-to-all | bytes 262144 | tf_op jit(solution)/shard_map/all_to_all | solution.py:287
  76.1 0.7 copy_bitcast_fusion
  (1 shorter events, 0.0 us)
Async XLA Ops:
  2.6 33.2 %all-to-all-start = ((bf16[32,25,2,128]{3,2,1,0:T(2,128)(2,1)}), bf16[32,25,2,128]{3,2,1,0:T(2,128)(2,1)S(1)}, u32[]{:S(2)}, u32[]{:S(2)}) async-start(bf16[32,25,2,128]{3,2,1,0:T(2,128)(2,1)} %shard_map.68), calls=%async_computation | async-start | bytes 819200 | tf_op jit(solution)/shard_map/all_to_all | solution.py:271
  47.3 7.7 %collective-permute-start = (f32[128,256]{1,0:T(8,128)S(1)}, f32[128,256]{1,0:T(8,128)S(1)}, u32[]{:S(2)}, u32[]{:S(2)}) collective-permute-start(f32[128,256]{1,0:T(8,128)S(1)} %get-tuple-element.13), channel_id=1, source_target_pairs={{0,128},{64,192},{128,256},{32,288},{192,320},{96,352},{256,384},{... | collective-permute-start | bytes 393224 | tf_op jit(solution)/shard_map/ppermute | solution.py:280
  50.5 6.6 %collective-permute-start.1 = (f32[128,128]{1,0:T(8,128)S(1)}, f32[128,128]{1,0:T(8,128)S(1)}, u32[]{:S(2)}, u32[]{:S(2)}) collective-permute-start(f32[128,128]{1,0:T(8,128)S(1)} %slice.3), channel_id=1, source_target_pairs={{0,384},{32,416},{64,448},{96,480},{1,385},{33,417},{65,449},{97,4... | collective-permute-start | bytes 196616 | tf_op jit(solution)/shard_map/ppermute | solution.py:266

commit v6 on v5

--- a/solution.py
+++ b/solution.py
@@ -173,11 +173,12 @@
     eye = jnp.where(apart == 0, 1.0, 0.0)
     n1 = [jnp.where(apart < 16, -b, 0.0) for b in blocks]
     n2 = [dot_pair(n, n) for n in n1]
-    x = [eye + n + m + dot_pair(n, m) for n, m in zip(n1, n2)]
-    n4 = [dot_pair(n, n) for n in n2]
-    x = [y + dot_pair(y, n) for y, n in zip(x, n4)]
-    n8 = [dot_pair(n, n) for n in n4]
-    x = [y + dot_pair(y, n) for y, n in zip(x, n8)]
+    both = [dot_pair(jnp.concatenate([n, m], axis=0), m) for n, m in zip(n1, n2)]
+    x = [eye + n + m + t[:DIM] for n, m, t in zip(n1, n2, both)]
+    n4 = [t[DIM:] for t in both]
+    both = [dot_pair(jnp.concatenate([y, n], axis=0), n) for y, n in zip(x, n4)]
+    x = [y + t[:DIM] for y, t in zip(x, both)]
+    x = [y + dot_pair(y, t[DIM:]) for y, t in zip(x, both)]
     for width in (16, 32, 64):
         here = picked(apart, width)
         here = (here >= width) & (here < 2 * width)
@@ -221,8 +222,8 @@
         direct_ref[span, :] = mixed[:, DIM:] + step[:, DIM:]
 
 
-def group_kernel(spot_ref, group_ref, before_ref, upto_ref, total_ref):
-    spot = spot_ref[0]
+def group_kernel(group_ref, before_ref, upto_ref, total_ref):
+    spot = lax.axis_index("seq") % 4
     d_row, d_col = iota((DIM, 2 * DIM), 0), iota((DIM, 2 * DIM), 1)
     first = group_ref[0]
     two = after(group_ref[1], first)
@@ -274,8 +275,7 @@
     count = lax.axis_size("seq")
     groups = [list(range(first, first + 4)) for first in range(0, count, 4)]
     group = lax.all_gather(own, "seq", axis_index_groups=groups)
-    spot = (lax.axis_index("seq") % 4).astype(jnp.int32)[None]
-    before, upto, total = call(group_kernel, pair, pair, pair)(spot, group)
+    before, upto, total = call(group_kernel, pair, pair, pair)(group)
     route = [(i - 4 * (1 + i % 2), i) for i in range(count) if i >= 4 * (1 + i % 2)]
     mixed = lax.ppermute(total, "seq", route)
     three = shifted(total[:, DIM:], 12)

time: 77.1 us -> 76.9 us (level)
  blocking collectives: 27 us -> 60.3 us
  waiting for transfers between devices: 19 us -> 1.77 us
  starting transfers between devices: 19.7 us -> 3.78 us
    all_to_all x0 -> x1, blocking collectives: none -> 33.2 us  [per_device(): lax.all_to_all(packed, 'head', split_axis=0, concat_axis=0, tiled=True)]
    all_to_all x1 -> x0, waiting for transfers between devices: 17.2 us -> none  [per_device(): lax.all_to_all(packed, 'head', split_axis=0, concat_axis=0, tiled=True)]
    all_to_all x1 -> x0, starting transfers between devices: 16 us -> none  [per_device(): lax.all_to_all(packed, 'head', split_axis=0, concat_axis=0, tiled=True)]
  transfers between devices with their start and end apart: 3 -> 2, of which waited for: 2 -> 1; matrix products, arithmetic and copies ran while one was open for 0% -> 0% of each run, Pallas kernels for 3% -> 3%
where the time goes in v6:
time: 76.9 us; the launch traced here: 76.6 us
  blocking collectives  60.3 us (78%)
  Pallas kernels  9.42 us (12%)
  starting transfers between devices  3.78 us (5%)
  waiting for transfers between devices  1.77 us (2%)
    all_to_all x1, blocking collectives, per_device(): lax.all_to_all(packed, 'head', split_axis=0, concat_axis=0, tiled=True)  33.2 us
    all_to_all x1, blocking collectives, per_device(): lax.all_to_all(rows, 'head', split_axis=0, concat_axis=1, tiled=True)  17.8 us
    pallas_call x4, Pallas kernels, run(): pl.pallas_call(kernel, out_shape=outs, in_specs=[pl.BlockSpec(memory_spac...  7.45 us
    all_gather x1, blocking collectives, per_device(): group = lax.all_gather(own, 'seq', axis_index_groups=groups)  7.15 us
    ppermute x1, starting transfers between devices, per_device(): mixed = lax.ppermute(total, 'seq', route)  3.11 us
    all_gather x1, blocking collectives, per_device(): lax.all_gather(mixed, 'seq', axis_index_groups=[[i, i + 1] for i in range...  2.14 us
    pallas_call x1, Pallas kernels, pack(): pl.pallas_call(pack_kernel, out_shape=jax.ShapeDtypeStruct((SRC, 25, 2, D...  1.97 us
    ppermute x1, waiting for transfers between devices, per_device(): mixed = lax.ppermute(total, 'seq', route)  1.77 us
  transfers between devices with their start and end apart: 2, of which 1 were waited for; matrix products, arithmetic and copies ran while one was open for 0% of the time, Pallas kernels for 3%

profile of v6, /device:TPU:4, one launch (start us, length us, event | category | flops | bytes accessed | tf_op | source)
XLA Modules:
  0.0 76.6 jit_solution(6894390060085421470)
XLA Ops:
  0.6 2.0 %shard_map.68 = bf16[32,25,2,128]{3,2,1,0:T(2,128)(2,1)} custom-call(bf16[16,16,128]{2,1,0:T(8,128)(2,1)} %refs_0_.1, bf16[16,16,128]{2,1,0:T(8,128)(2,1)} %refs_1_.1, bf16[16,32,128]{2,1,0:T(8,128)(2,1)} %refs_2_.1, bf16[16,32]{1,0:T(8,128)(2,1)} %refs_3_.1, bf16[16,32]{1,0:T(8,128)(2,1)} %refs_4_.1), custom_call_target="tpu_custom_call" | custom-call | tf_op jit(solution)/shard_map/pallas_call | solution.py:98
  2.6 33.2 %all_to_all.24.got_ref = bf16[32,25,2,128]{3,2,1,0:T(2,128)(2,1)S(1)} all-to-all(bf16[32,25,2,128]{3,2,1,0:T(2,128)(2,1)} %shard_map.68), channel_id=1, replica_groups=mesh['seq'=16,'head'=32] {'head'}, dimensions={0} | all-to-all | bytes 819200 | tf_op jit(solution)/shard_map/all_to_all | solution.py:272
  35.8 3.9 %shard_map.69 = (f32[128,256]{1,0:T(8,128)S(1)}, f32[512,256]{1,0:T(8,128)S(1)}, f32[3,128,256]{2,1,0:T(8,128)S(1)}) custom-call(bf16[32,25,2,128]{3,2,1,0:T(2,128)(2,1)S(1)} %all_to_all.24.got_ref), custom_call_target="tpu_custom_call" | custom-call | tf_op jit(solution)/shard_map/pallas_call | solution.py:252
  39.6 7.1 %all-gather = f32[512,256]{1,0:T(8,128)S(1)} all-gather(f32[128,256]{1,0:T(8,128)S(1)} %get-tuple-element.12), channel_id=2, replica_groups={{0,32,64,96},{128,160,192,224},{256,288,320,352},{384,416,448,480},{1,3..., dimensions={0}, use_global_device_ids=true | all-gather | bytes 655360 | tf_op jit(solution)/shard_map/all_gather | solution.py:277
  46.8 0.4 shard_map.70
  47.2 3.1 %collective-permute-start = (f32[128,256]{1,0:T(8,128)S(1)}, f32[128,256]{1,0:T(8,128)S(1)}, u32[]{:S(2)}, u32[]{:S(2)}) collective-permute-start(f32[128,256]{1,0:T(8,128)S(1)} %get-tuple-element.13), channel_id=1, source_target_pairs={{0,128},{64,192},{128,256},{32,288},{192,320},{96,352},{256,384},{... | collective-permute-start | bytes 393224 | tf_op jit(solution)/shard_map/ppermute | solution.py:280
  50.4 0.7 collective-permute-start.1
  51.0 2.0 %shard_map.71 = (f32[512,128]{1,0:T(8,128)S(1)}, f32[512,128]{1,0:T(8,128)S(1)}) custom-call(bf16[32,25,2,128]{3,2,1,0:T(2,128)(2,1)S(1)} %all_to_all.24.got_ref, f32[512,256]{1,0:T(8,128)S(1)} %get-tuple-element.15.solved_ref, f32[3,128,256]{2,1,0:T(8,128)S(1)} %get-tuple-element.16.maps_ref, f32[128,256]{1,0:T(8,128)S(1)} %get-tuple-element.17.before_ref), custom_call_target="tpu_custom_call" | custom-call | tf_op jit(solution)/shard_map/pallas_call | solution.py:252
  53.0 1.8 %collective-permute-done = f32[128,256]{1,0:T(8,128)S(1)} collective-permute-done((f32[128,256]{1,0:T(8,128)S(1)}, f32[128,256]{1,0:T(8,128)S(1)}, u32[]{:S(2)}, u32[]{:S(2)}) %collective-permute-start) | collective-permute-done | bytes 131104 | tf_op jit(solution)/shard_map/ppermute | solution.py:280
  54.8 2.1 %all-gather.1 = f32[256,256]{1,0:T(8,128)S(1)} all-gather(f32[128,256]{1,0:T(8,128)S(1)} %collective-permute-done), channel_id=3, replica_groups={{0,32},{64,96},{128,160},{192,224},{256,288},{320,352},{384,416},{448,4..., dimensions={0}, use_global_device_ids=true | all-gather | bytes 393216 | tf_op jit(solution)/shard_map/all_gather | solution.py:283
  56.9 0.0 collective-permute-done.1.three_ref
  56.9 1.2 %shard_map.72 = (bf16[512,128]{1,0:T(8,128)(2,1)S(1)}, f32[128,128]{1,0:T(8,128)}) custom-call(f32[2,128,256]{2,1,0:T(8,128)S(1)} %bitcast.11, f32[128,128]{1,0:T(8,128)S(1)} %collective-permute-done.1.three_ref, f32[128,256]{1,0:T(8,128)S(1)} %get-tuple-element.14.upto_ref, f32[512,128]{1,0:T(8,128)S(1)} %get-tuple-element.18.direct_ref, ...), custom_call_target="tpu_custom_call" | custom-call | tf_op jit(solution)/shard_map/pallas_call | solution.py:252
  58.1 17.8 %all_to_all.25 = bf16[32,16,128]{2,1,0:T(8,128)(2,1)S(1)} all-to-all(bf16[32,16,128]{2,1,0:T(8,128)(2,1)S(1)} %bitcast.12), channel_id=1, replica_groups=mesh['seq'=16,'head'=32] {'head'}, dimensions={0} | all-to-all | bytes 262144 | tf_op jit(solution)/shard_map/all_to_all | solution.py:287
  76.0 0.7 copy_bitcast_fusion
  (1 shorter events, 0.0 us)
Async XLA Ops:
  47.2 7.6 %collective-permute-start = (f32[128,256]{1,0:T(8,128)S(1)}, f32[128,256]{1,0:T(8,128)S(1)}, u32[]{:S(2)}, u32[]{:S(2)}) collective-permute-start(f32[128,256]{1,0:T(8,128)S(1)} %get-tuple-element.13), channel_id=1, source_target_pairs={{0,128},{64,192},{128,256},{32,288},{192,320},{96,352},{256,384},{... | collective-permute-start | bytes 393224 | tf_op jit(solution)/shard_map/ppermute | solution.py:280
  50.4 6.6 %collective-permute-start.1 = (f32[128,128]{1,0:T(8,128)S(1)}, f32[128,128]{1,0:T(8,128)S(1)}, u32[]{:S(2)}, u32[]{:S(2)}) collective-permute-start(f32[128,128]{1,0:T(8,128)S(1)} %slice.3), channel_id=1, source_target_pairs={{0,384},{32,416},{64,448},{96,480},{1,385},{33,417},{65,449},{97,4... | collective-permute-start | bytes 196616 | tf_op jit(solution)/shard_map/ppermute | solution.py:267

commit v7 on v6

--- a/solution.py
+++ b/solution.py
@@ -238,11 +238,26 @@
     total_ref[...] = chain[4]
 
 
-def last_kernel(near_ref, three_ref, upto_ref, direct_ref, reach_ref, out_ref, state_ref):
+def last_kernel(near_ref, three_ref, upto_ref, direct_ref, reach_ref, out_ref, state_ref, state, sem):
     arriving = dot_pair(near_ref[1, :, :DIM], three_ref[...]) + near_ref[1, :, DIM:]
     arriving = dot_pair(near_ref[0, :, :DIM], arriving) + near_ref[0, :, DIM:]
-    state_ref[...] = dot_pair(upto_ref[:, :DIM], arriving) + upto_ref[:, DIM:]
+    state[...] = dot_pair(upto_ref[:, :DIM], arriving) + upto_ref[:, DIM:]
+    copy = pltpu.make_async_copy(state, state_ref, sem)
+    copy.start()
     out_ref[...] = (direct_ref[...] + dot_pair(reach_ref[...], arriving)).astype(BF16)
+    copy.wait()
+
+
+def finish(*operands):
+    vmem = pl.BlockSpec(memory_space=pltpu.VMEM)
+    return pl.pallas_call(
+        last_kernel,
+        out_shape=(jax.ShapeDtypeStruct((TOK, DIM), BF16), jax.ShapeDtypeStruct((DIM, DIM), F32)),
+        in_specs=[vmem] * len(operands),
+        out_specs=(vmem, pl.BlockSpec(memory_space=pl.ANY)),
+        scratch_shapes=[pltpu.VMEM((DIM, DIM), F32), pltpu.SemaphoreType.DMA],
+        compiler_params=pltpu.CompilerParams(vmem_limit_bytes=48 << 20),
+    )(*operands)
 
 
 def call(kernel, *shapes):
@@ -281,9 +296,7 @@
     three = shifted(total[:, DIM:], 12)
     direct, reach = call(readout_kernel, ((TOK, DIM), F32), ((TOK, DIM), F32))(got, solved, maps, before)
     near = lax.all_gather(mixed, "seq", axis_index_groups=[[i, i + 1] for i in range(0, count, 2)])
-    rows, last_state = call(last_kernel, ((TOK, DIM), BF16), ((DIM, DIM), F32))(
-        near, three, upto, direct, reach
-    )
+    rows, last_state = finish(near, three, upto, direct, reach)
     head_output = lax.all_to_all(rows, "head", split_axis=0, concat_axis=1, tiled=True)
     return head_output, last_state[None, None]
 

time: 76.9 us -> 77 us (level)
    pallas_call x0 -> x1, Pallas kernels: none -> 1.18 us  [finish(): pl.pallas_call(last_kernel, out_shape=(jax.ShapeDtypeStruct((TOK, DIM), B...]
    pallas_call x4 -> x3, Pallas kernels: 7.45 us -> 6.28 us  [run(): pl.pallas_call(kernel, out_shape=outs, in_specs=[pl.BlockSpec(memory_spac...]
where the time goes in v7:
time: 77 us; the launch traced here: 76.6 us
  blocking collectives  60.3 us (78%)
  Pallas kernels  9.42 us (12%)
  starting transfers between devices  3.78 us (5%)
  waiting for transfers between devices  1.77 us (2%)
    all_to_all x1, blocking collectives, per_device(): lax.all_to_all(packed, 'head', split_axis=0, concat_axis=0, tiled=True)  33.2 us
    all_to_all x1, blocking collectives, per_device(): lax.all_to_all(rows, 'head', split_axis=0, concat_axis=1, tiled=True)  17.9 us
    all_gather x1, blocking collectives, per_device(): group = lax.all_gather(own, 'seq', axis_index_groups=groups)  7.15 us
    pallas_call x3, Pallas kernels, run(): pl.pallas_call(kernel, out_shape=outs, in_specs=[pl.BlockSpec(memory_spac...  6.28 us
    ppermute x1, starting transfers between devices, per_device(): mixed = lax.ppermute(total, 'seq', route)  3.11 us
    all_gather x1, blocking collectives, per_device(): lax.all_gather(mixed, 'seq', axis_index_groups=[[i, i + 1] for i in range...  2.14 us
    pallas_call x1, Pallas kernels, pack(): pl.pallas_call(pack_kernel, out_shape=jax.ShapeDtypeStruct((SRC, 25, 2, D...  1.97 us
    ppermute x1, waiting for transfers between devices, per_device(): mixed = lax.ppermute(total, 'seq', route)  1.77 us
  transfers between devices with their start and end apart: 2, of which 1 were waited for; matrix products, arithmetic and copies ran while one was open for 0% of the time, Pallas kernels for 3%

profile of v7, /device:TPU:4, one launch (start us, length us, event | category | flops | bytes accessed | tf_op | source)
XLA Modules:
  0.0 76.6 jit_solution(12619188820880810837)
XLA Ops:
  0.6 2.0 %shard_map.68 = bf16[32,25,2,128]{3,2,1,0:T(2,128)(2,1)} custom-call(bf16[16,16,128]{2,1,0:T(8,128)(2,1)} %refs_0_.1, bf16[16,16,128]{2,1,0:T(8,128)(2,1)} %refs_1_.1, bf16[16,32,128]{2,1,0:T(8,128)(2,1)} %refs_2_.1, bf16[16,32]{1,0:T(8,128)(2,1)} %refs_3_.1, bf16[16,32]{1,0:T(8,128)(2,1)} %refs_4_.1), custom_call_target="tpu_custom_call" | custom-call | tf_op jit(solution)/shard_map/pallas_call | solution.py:98
  2.6 33.2 %all_to_all.24.got_ref = bf16[32,25,2,128]{3,2,1,0:T(2,128)(2,1)S(1)} all-to-all(bf16[32,25,2,128]{3,2,1,0:T(2,128)(2,1)} %shard_map.68), channel_id=1, replica_groups=mesh['seq'=16,'head'=32] {'head'}, dimensions={0} | all-to-all | bytes 819200 | tf_op jit(solution)/shard_map/all_to_all | solution.py:287
  35.8 3.9 %shard_map.69 = (f32[128,256]{1,0:T(8,128)S(1)}, f32[512,256]{1,0:T(8,128)S(1)}, f32[3,128,256]{2,1,0:T(8,128)S(1)}) custom-call(bf16[32,25,2,128]{3,2,1,0:T(2,128)(2,1)S(1)} %all_to_all.24.got_ref), custom_call_target="tpu_custom_call" | custom-call | tf_op jit(solution)/shard_map/pallas_call | solution.py:267
  39.6 7.1 %all-gather = f32[512,256]{1,0:T(8,128)S(1)} all-gather(f32[128,256]{1,0:T(8,128)S(1)} %get-tuple-element.12), channel_id=2, replica_groups={{0,32,64,96},{128,160,192,224},{256,288,320,352},{384,416,448,480},{1,3..., dimensions={0}, use_global_device_ids=true | all-gather | bytes 655360 | tf_op jit(solution)/shard_map/all_gather | solution.py:292
  46.8 0.4 shard_map.70
  47.2 3.1 %collective-permute-start = (f32[128,256]{1,0:T(8,128)S(1)}, f32[128,256]{1,0:T(8,128)S(1)}, u32[]{:S(2)}, u32[]{:S(2)}) collective-permute-start(f32[128,256]{1,0:T(8,128)S(1)} %get-tuple-element.13), channel_id=1, source_target_pairs={{0,128},{64,192},{128,256},{32,288},{192,320},{96,352},{256,384},{... | collective-permute-start | bytes 393224 | tf_op jit(solution)/shard_map/ppermute | solution.py:295
  50.4 0.7 collective-permute-start.1
  51.0 2.0 %shard_map.71 = (f32[512,128]{1,0:T(8,128)S(1)}, f32[512,128]{1,0:T(8,128)S(1)}) custom-call(bf16[32,25,2,128]{3,2,1,0:T(2,128)(2,1)S(1)} %all_to_all.24.got_ref, f32[512,256]{1,0:T(8,128)S(1)} %get-tuple-element.15.solved_ref, f32[3,128,256]{2,1,0:T(8,128)S(1)} %get-tuple-element.16.maps_ref, f32[128,256]{1,0:T(8,128)S(1)} %get-tuple-element.17.before_ref), custom_call_target="tpu_custom_call" | custom-call | tf_op jit(solution)/shard_map/pallas_call | solution.py:267
  53.0 1.8 %collective-permute-done = f32[128,256]{1,0:T(8,128)S(1)} collective-permute-done((f32[128,256]{1,0:T(8,128)S(1)}, f32[128,256]{1,0:T(8,128)S(1)}, u32[]{:S(2)}, u32[]{:S(2)}) %collective-permute-start) | collective-permute-done | bytes 131104 | tf_op jit(solution)/shard_map/ppermute | solution.py:295
  54.8 2.1 %all-gather.1 = f32[256,256]{1,0:T(8,128)S(1)} all-gather(f32[128,256]{1,0:T(8,128)S(1)} %collective-permute-done), channel_id=3, replica_groups={{0,32},{64,96},{128,160},{192,224},{256,288},{320,352},{384,416},{448,4..., dimensions={0}, use_global_device_ids=true | all-gather | bytes 393216 | tf_op jit(solution)/shard_map/all_gather | solution.py:298
  56.9 0.0 collective-permute-done.1.three_ref
  56.9 1.2 %shard_map.72 = (bf16[512,128]{1,0:T(8,128)(2,1)S(1)}, f32[128,128]{1,0:T(8,128)}) custom-call(f32[2,128,256]{2,1,0:T(8,128)S(1)} %bitcast.11, f32[128,128]{1,0:T(8,128)S(1)} %collective-permute-done.1.three_ref, f32[128,256]{1,0:T(8,128)S(1)} %get-tuple-element.14.upto_ref, f32[512,128]{1,0:T(8,128)S(1)} %get-tuple-element.18.direct_ref, ...), custom_call_target="tpu_custom_call" | custom-call | tf_op jit(solution)/shard_map/pallas_call | solution.py:253
  58.1 17.9 %all_to_all.25 = bf16[32,16,128]{2,1,0:T(8,128)(2,1)S(1)} all-to-all(bf16[32,16,128]{2,1,0:T(8,128)(2,1)S(1)} %bitcast.12), channel_id=1, replica_groups=mesh['seq'=16,'head'=32] {'head'}, dimensions={0} | all-to-all | bytes 262144 | tf_op jit(solution)/shard_map/all_to_all | solution.py:300
  76.0 0.7 copy_bitcast_fusion
  (1 shorter events, 0.0 us)
Async XLA Ops:
  47.2 7.6 %collective-permute-start = (f32[128,256]{1,0:T(8,128)S(1)}, f32[128,256]{1,0:T(8,128)S(1)}, u32[]{:S(2)}, u32[]{:S(2)}) collective-permute-start(f32[128,256]{1,0:T(8,128)S(1)} %get-tuple-element.13), channel_id=1, source_target_pairs={{0,128},{64,192},{128,256},{32,288},{192,320},{96,352},{256,384},{... | collective-permute-start | bytes 393224 | tf_op jit(solution)/shard_map/ppermute | solution.py:295
  50.4 6.6 %collective-permute-start.1 = (f32[128,128]{1,0:T(8,128)S(1)}, f32[128,128]{1,0:T(8,128)S(1)}, u32[]{:S(2)}, u32[]{:S(2)}) collective-permute-start(f32[128,128]{1,0:T(8,128)S(1)} %slice.3), channel_id=1, source_target_pairs={{0,384},{32,416},{64,448},{96,480},{1,385},{33,417},{65,449},{97,4... | collective-permute-start | bytes 196616 | tf_op jit(solution)/shard_map/ppermute | solution.py:282
